TPU v7x, 128 devices: a whole 4x4x4 slice. The times are simulated.
128 devices in a mesh: mem: 4 (over x_hi, core), tile: 32 (over x_lo, y, z).
Axes of the slice: x: 4 (x_hi: 2, x_lo: 2; x = x_hi * 2 + x_lo), y: 4, z: 4, core: 2. Of those that a mesh axis runs over, the one named last changes fastest.
Arguments:
- latents: float32 [24, 256], P('mem'), may hold values from -6 to 6
- basis: bfloat16 [256, 2, 512, 512], P(None, None, 'tile'), may hold values from -0.375 to 0.375
- conv_in: bfloat16 [9, 64], replicated, may hold values from -2 to 2
- conv_mid: bfloat16 [9, 64, 64], replicated, may hold values from -0.25 to 0.25
- conv_out: bfloat16 [64], replicated, may hold values from -0.75 to 0.75
- pressure_prev: float32 [2, 512, 512], P(None, 'tile'), may hold values from -6 to 6
- source: float32 [2, 512, 512], P(None, 'tile'), may hold values from -6 to 6
- perf_cells: int32 [384, 8], replicated, may hold values from 0 to 524287
- perf_count: int32 [384], replicated, may hold values from 1 to 8
- obs_perturbed: float32 [24, 384], replicated, may hold values from -6 to 6
- obs_error: float32 [384], replicated, may hold values from 0.2 to 2
Outputs:
- pressure: float32 [24, 2, 512, 512], P(None, None, 'tile', 'mem')
- well_data: float32 [24, 384], replicated
- latents_new: float32 [24, 256], P('mem')
All inputs are finite; a program needn't handle non-finite values.
Results may differ from a plain program's by a relative error of at most 0.0055.
Values may be sent and summed in bfloat16 or wider, within the bound.
A program may use at most 128 MiB of HBM per device.

v0:
```python
import math

import jax
import jax.numpy as jnp
from jax import lax
from jax.sharding import PartitionSpec as P

SWEEPS = 2


storage_coef = 1.0


def extended(cells, sides, width):
    for axis, dim in sides:
        count = lax.axis_size(axis)
        ends = count - 1
        head = lax.slice_in_dim(cells, 0, width, axis=dim)
        tail = lax.slice_in_dim(cells, cells.shape[dim] - width, cells.shape[dim], axis=dim)
        cells = jnp.concatenate(
            [
                lax.ppermute(tail, axis, [(i, (i + 1) % count) for i in range(ends)]),
                cells,
                lax.ppermute(head, axis, [((i + 1) % count, i) for i in range(ends)]),
            ],
            axis=dim,
        )
    return cells


def lift(field, conv_in):
    rows = field.shape[1] - 2
    width = field.shape[2]
    padded = jnp.pad(field, ((0, 0), (0, 0), (1, 1)))
    total = jnp.zeros((field.shape[0], conv_in.shape[1], rows, width), jnp.float32)
    for tap in range(9):
        part = padded[:, tap // 3 : tap // 3 + rows, tap % 3 : tap % 3 + width]
        total = total + conv_in[tap].astype(jnp.float32)[None, :, None, None] * part[:, None]
    return jax.nn.relu(total).astype(jnp.bfloat16)


def mix(lifted, field, conv_mid, conv_out):
    rows = field.shape[1]
    width = field.shape[2]
    padded = jnp.pad(lifted, ((0, 0), (0, 0), (0, 0), (1, 1)))
    total = jnp.zeros((field.shape[0], conv_mid.shape[1], rows, width), jnp.float32)
    for tap in range(9):
        part = padded[:, :, tap // 3 : tap // 3 + rows, tap % 3 : tap % 3 + width]
        total = total + jnp.einsum(
            "oc,zcxy->zoxy", conv_mid[tap], part, preferred_element_type=jnp.float32
        )
    deep = jax.nn.relu(total)
    return field + jnp.einsum("c,zcxy->zxy", conv_out.astype(jnp.float32), deep)


def neighbours(wide):
    zpad = jnp.pad(wide, ((0, 0), (1, 1), (0, 0), (0, 0)))
    return [
        zpad[:, 1:-1, 2:, 1:-1],
        zpad[:, 1:-1, :-2, 1:-1],
        zpad[:, 1:-1, 1:-1, 2:],
        zpad[:, 1:-1, 1:-1, :-2],
        zpad[:, 2:, 1:-1, 1:-1],
        zpad[:, :-2, 1:-1, 1:-1],
    ]


def well_terms(perm, press, perf_cells, perf_count, row_start, col_start, grid_rows, grid_cols):
    members = perm.shape[0]
    rows = perm.shape[2]
    width = perm.shape[3]
    wells = perf_cells.shape[0]
    slots = perf_cells.shape[1]
    ids = perf_cells.reshape(-1)
    layer_of = ids // (grid_rows * grid_cols)
    rest = ids % (grid_rows * grid_cols)
    row_local = rest // grid_cols - row_start
    col_local = rest % grid_cols - col_start
    inside = (row_local >= 0) & (row_local < rows) & (col_local >= 0) & (col_local < width)
    local_ids = jnp.where(inside, layer_of * rows * width + row_local * width + col_local, 0)
    used = (jnp.arange(slots)[None, :] < perf_count[:, None]).reshape(-1) & inside
    weight = used.astype(jnp.float32)
    perm_at = jnp.take(perm.reshape(members, -1), local_ids, axis=1) * weight[None, :]
    press_at = jnp.take(press.reshape(members, -1), local_ids, axis=1)
    numer = jnp.sum((perm_at * press_at).reshape(members, wells, slots), axis=2)
    weight_sum = jnp.sum(perm_at.reshape(members, wells, slots), axis=2)
    return (numer, weight_sum)


def body(
    latents,
    basis,
    conv_in,
    conv_mid,
    conv_out,
    pressure_prev,
    source,
    perf_cells,
    perf_count,
    obs_perturbed,
    obs_error,
):
    mem_dev = latents.shape[0]
    layers = basis.shape[1]
    rows = basis.shape[2]
    width = basis.shape[3]
    tile_at = lax.axis_index("tile")
    mem_at = lax.axis_index("mem")
    grid_rows = rows * lax.axis_size("tile")
    flat_basis = basis.reshape(basis.shape[0], -1)
    field = jnp.dot(latents.astype(jnp.bfloat16), flat_basis, preferred_element_type=jnp.float32)
    field = field.reshape(mem_dev, layers, rows, width)
    wide = extended(field, (("tile", 2),), 1)
    lifted = lax.map(lambda single: lift(single, conv_in), wide)
    lifted_wide = extended(lifted, (("tile", 3),), 1)
    log_perm = lax.map(lambda pair: mix(pair[0], pair[1], conv_mid, conv_out), (lifted_wide, field))
    base_full = storage_coef * pressure_prev + source
    log_tiles = lax.all_to_all(log_perm, "mem", split_axis=3, concat_axis=0, tiled=True)
    cols = log_tiles.shape[3]
    perm = jnp.exp(log_tiles)
    base = lax.dynamic_slice_in_dim(base_full, mem_at * cols, cols, 2)
    prev_local = lax.dynamic_slice_in_dim(pressure_prev, mem_at * cols, cols, 2)
    perm_wide = extended(perm, (("mem", 3), ("tile", 2)), 1)
    conduct = [2.0 * perm * other / (perm + other) for other in neighbours(perm_wide)]
    denom = storage_coef + sum(conduct)
    press = jnp.broadcast_to(prev_local, perm.shape)
    for sweep in range(SWEEPS):
        press_wide = extended(press, (("mem", 3), ("tile", 2)), 1)
        acc = base[None] + sum((cval * nval for cval, nval in zip(conduct, neighbours(press_wide))))
        press = acc / denom
    numer, weight_sum = well_terms(
        perm,
        press,
        perf_cells,
        perf_count,
        tile_at * rows,
        mem_at * cols,
        grid_rows,
        cols * lax.axis_size("mem"),
    )
    members = press.shape[0]
    numer, weight_sum = lax.psum((numer, weight_sum), ("mem", "tile"))
    well_data = numer / weight_sum
    scale = 2.0 * obs_error
    centred = well_data - jnp.mean(well_data, axis=0, keepdims=True)
    scaled = centred / (math.sqrt(members - 1) * scale[None, :])
    innov = (obs_perturbed - well_data) / scale[None, :]
    gram = jnp.eye(members, dtype=jnp.float32) + jnp.dot(
        scaled, scaled.T, precision=lax.Precision.HIGHEST
    )
    cross = jnp.dot(scaled, innov.T, precision=lax.Precision.HIGHEST)
    factor = jnp.linalg.cholesky(gram)
    weights = jax.scipy.linalg.cho_solve((factor, True), cross)
    every = lax.all_gather(latents, "mem", axis=0, tiled=True)
    spread = (every - jnp.mean(every, axis=0, keepdims=True)) / math.sqrt(members - 1)
    own_weights = lax.dynamic_slice_in_dim(weights, mem_at * mem_dev, mem_dev, 1)
    latents_new = latents + jnp.dot(own_weights.T, spread, precision=lax.Precision.HIGHEST)
    return (press, well_data, latents_new)


def solution(mesh):
    return jax.shard_map(
        body,
        mesh=mesh,
        in_specs=(
            P("mem", None),
            P(None, None, "tile", None),
            P(),
            P(),
            P(),
            P(None, "tile", None),
            P(None, "tile", None),
            P(),
            P(),
            P(),
            P(),
        ),
        out_specs=(P(None, None, "tile", "mem"), P(), P("mem", None)),
        check_vma=False,
    )
```

profile of v0, /device:TPU:1, one launch (start us, length us, event | category | flops | bytes accessed | tf_op | source)
XLA Modules:
  0.0 651.2 jit_solution(13168219996132069656)
XLA Ops:
  7.2 15.4 %copy.59 = bf16[32,8,32,512]{3,1,2,0:T(8,128)(2,1)} copy(bf16[32,8,32,512]{3,2,1,0:T(8,128)(2,1)} %bitcast.226) | data formatting | bytes 16777216
  22.6 11.9 %copy.29 = bf16[16384,256]{1,0:T(8,128)(2,1)} copy(bf16[16384,256]{0,1:T(8,128)(2,1)} %bitcast.222) | data formatting | bytes 16777216 | tf_op jit(solution)/shard_map/dot_general | solution.py:111
  34.5 5.6 fusion.110
  49.4 35.6 %while.24 = (s32[]{:T(128)}, bf16[6,2,64,16,512]{4,2,3,1,0:T(8,128)(2,1)}, bf16[9,64]{1,0:T(8,128)(2,1)S(1)}, f32[6,2,18,512]{3,0,2,1:T(8,128)S(1)}, s32[]{:T(128)}) while((s32[]{:T(128)}, bf16[6,2,64,16,512]{4,2,3,1,0:T(8,128)(2,1)}, bf16[9,64]{1,0:T(8,128)(2,1)S(1)}, f32[6,2,18,512]{3,0,2,1:T(8,128)S(1)}, s32[]{:T(128)}) %tuple.105), condition=%wide.region_1.2_spmd, body=%wide.region_0.1_spmd.sunk | while | flops 19923520 | bytes 8067265 | solution.py:114
  93.6 6.9 %collective-permute-start.7 = (f32[24,2,16,1]{3,2,1,0:T(8,128)}, f32[24,2,16,1]{3,2,1,0:T(8,128)}, u32[]{:S(2)}, u32[]{:S(2)}) collective-permute-start(f32[24,2,16,1]{3,2,1,0:T(8,128)} %broadcast_in_dim.48), channel_id=1, source_target_pairs={{0,32},{32,64},{64,96},{1,33},{33,65},{65,97},{2,34},{34,66},{66,9... | collective-permute-start | bytes 9224 | tf_op jit(solution)/shard_map/ppermute | solution.py:22
  110.0 10.3 %pad_maximum_fusion = bf16[6,2,64,18,512]{4,2,3,1,0:T(8,128)(2,1)} fusion(bf16[6,2,64,1,512]{4,2,3,1,0:T(8,128)(2,1)S(1)} %collective-permute-done.3, bf16[6,2,64,16,512]{4,2,3,1,0:T(8,128)(2,1)} %get-tuple-element.134, bf16[6,2,64,1,512]{4,2,3,1,0:T(8,128)(2,1)S(1)} %collective-permute-done.2), kind=kLoop, calls=%fused_computation.83 | loop fusion | flops 14155776 | bytes 28311552 | tf_op jit(solution)/shard_map/concatenate | solution.py:20
  120.3 224.6 %while.25 = (s32[]{:T(128)}, f32[6,2,16,512]{3,2,1,0:T(8,128)S(1)}, f32[6,2,16,512]{3,0,2,1:T(8,128)S(1)}, bf16[6,2,64,18,512]{4,2,3,1,0:T(8,128)(2,1)}, bf16[9,...) while((s32[]{:T(128)}, f32[6,2,16,512]{3,2,1,0:T(8,128)S(1)}, ...), condition=%wide.region_3.4_spmd, body=%wide.region_2.3_spmd.sunk | while | flops 1219510272 | bytes 92815952 | solution.py:116
  144.2 13.4 %fusion.170 = f32[1,2,16,512]{3,0,2,1:T(1,128)S(1)} fusion(f32[2,16,512,64]{2,3,1,0:T(8,128)} %fusion.162, f32[2,16,512,64]{2,3,1,0:T(8,128)} %fusion.163, f32[2,16,512,64]{2,3,1,0:T(8,128)} %fusion.164, f32[2,16,512,64]{2,3,1,0:T(8,128)} %fusion.165, f32[2,16,512,64]{2,3,1,0:T(8,128)} %fusion.166, f32[2,16,512,64]{2,3,1,0:T(8,128)} %fusion.167, ...), kind=kOutput, calls=%fused_computation.21.clone.1 | convolution fusion | flops 145752064 | bytes 35996160 | tf_op jit(solution)/shard_map/while/body/eval_jaxpr/c,zcxy->zxy/dot_general | solution.py:53
  181.7 13.4 %fusion.170 = f32[1,2,16,512]{3,0,2,1:T(1,128)S(1)} fusion(f32[2,16,512,64]{2,3,1,0:T(8,128)} %fusion.162, f32[2,16,512,64]{2,3,1,0:T(8,128)} %fusion.163, f32[2,16,512,64]{2,3,1,0:T(8,128)} %fusion.164, f32[2,16,512,64]{2,3,1,0:T(8,128)} %fusion.165, f32[2,16,512,64]{2,3,1,0:T(8,128)} %fusion.166, f32[2,16,512,64]{2,3,1,0:T(8,128)} %fusion.167, ...), kind=kOutput, calls=%fused_computation.21.clone.1 | convolution fusion | flops 145752064 | bytes 35996160 | tf_op jit(solution)/shard_map/while/body/eval_jaxpr/c,zcxy->zxy/dot_general | solution.py:53
  219.1 13.4 %fusion.170 = f32[1,2,16,512]{3,0,2,1:T(1,128)S(1)} fusion(f32[2,16,512,64]{2,3,1,0:T(8,128)} %fusion.162, f32[2,16,512,64]{2,3,1,0:T(8,128)} %fusion.163, f32[2,16,512,64]{2,3,1,0:T(8,128)} %fusion.164, f32[2,16,512,64]{2,3,1,0:T(8,128)} %fusion.165, f32[2,16,512,64]{2,3,1,0:T(8,128)} %fusion.166, f32[2,16,512,64]{2,3,1,0:T(8,128)} %fusion.167, ...), kind=kOutput, calls=%fused_computation.21.clone.1 | convolution fusion | flops 145752064 | bytes 35996160 | tf_op jit(solution)/shard_map/while/body/eval_jaxpr/c,zcxy->zxy/dot_general | solution.py:53
  256.6 13.4 %fusion.170 = f32[1,2,16,512]{3,0,2,1:T(1,128)S(1)} fusion(f32[2,16,512,64]{2,3,1,0:T(8,128)} %fusion.162, f32[2,16,512,64]{2,3,1,0:T(8,128)} %fusion.163, f32[2,16,512,64]{2,3,1,0:T(8,128)} %fusion.164, f32[2,16,512,64]{2,3,1,0:T(8,128)} %fusion.165, f32[2,16,512,64]{2,3,1,0:T(8,128)} %fusion.166, f32[2,16,512,64]{2,3,1,0:T(8,128)} %fusion.167, ...), kind=kOutput, calls=%fused_computation.21.clone.1 | convolution fusion | flops 145752064 | bytes 35996160 | tf_op jit(solution)/shard_map/while/body/eval_jaxpr/c,zcxy->zxy/dot_general | solution.py:53
  294.0 13.4 %fusion.170 = f32[1,2,16,512]{3,0,2,1:T(1,128)S(1)} fusion(f32[2,16,512,64]{2,3,1,0:T(8,128)} %fusion.162, f32[2,16,512,64]{2,3,1,0:T(8,128)} %fusion.163, f32[2,16,512,64]{2,3,1,0:T(8,128)} %fusion.164, f32[2,16,512,64]{2,3,1,0:T(8,128)} %fusion.165, f32[2,16,512,64]{2,3,1,0:T(8,128)} %fusion.166, f32[2,16,512,64]{2,3,1,0:T(8,128)} %fusion.167, ...), kind=kOutput, calls=%fused_computation.21.clone.1 | convolution fusion | flops 145752064 | bytes 35996160 | tf_op jit(solution)/shard_map/while/body/eval_jaxpr/c,zcxy->zxy/dot_general | solution.py:53
  331.4 13.4 %fusion.170 = f32[1,2,16,512]{3,0,2,1:T(1,128)S(1)} fusion(f32[2,16,512,64]{2,3,1,0:T(8,128)} %fusion.162, f32[2,16,512,64]{2,3,1,0:T(8,128)} %fusion.163, f32[2,16,512,64]{2,3,1,0:T(8,128)} %fusion.164, f32[2,16,512,64]{2,3,1,0:T(8,128)} %fusion.165, f32[2,16,512,64]{2,3,1,0:T(8,128)} %fusion.166, f32[2,16,512,64]{2,3,1,0:T(8,128)} %fusion.167, ...), kind=kOutput, calls=%fused_computation.21.clone.1 | convolution fusion | flops 145752064 | bytes 35996160 | tf_op jit(solution)/shard_map/while/body/eval_jaxpr/c,zcxy->zxy/dot_general | solution.py:53
  347.0 5.0 reshape.341
  352.0 7.6 %all-to-all-start = ((f32[4,1,24576]{2,1,0:T(1,128)}), f32[4,1,24576]{2,1,0:T(1,128)S(1)}, u32[]{:S(2)}, u32[]{:S(2)}) async-start(f32[4,1,24576]{2,1,0:T(1,128)} %reshape.341), calls=%async_computation | async-start | bytes 786432 | tf_op jit(solution)/shard_map/all_to_all | solution.py:118
  361.8 5.9 all-to-all-done
  404.6 4.8 fusion.71
  409.5 5.6 collective-permute-start.12
  419.8 5.9 collective-permute-done.13
  431.7 5.8 all-gather
  440.0 10.8 %gather_fusion = f32[3072,24]{1,0:T(8,128)} fusion(f32[24,4096]{0,1:T(8,128)S(1)} %copy.38, s32[3072]{0:T(1024)S(1)} %broadcast_clamp_fusion), kind=kCustom, calls=%fused_computation.clone | custom fusion | bytes 602112 | tf_op jit(solution)/shard_map/jit(_take)/gather | solution.py:83
  456.5 10.8 %gather_fusion.1 = f32[3072,24]{1,0:T(8,128)} fusion(f32[24,4096]{0,1:T(8,128)S(1)} %bitcast.225, s32[3072]{0:T(1024)S(1)} %broadcast_clamp_fusion), kind=kCustom, calls=%fused_computation.1.clone | custom fusion | bytes 602112 | tf_op jit(solution)/shard_map/jit(_take)/gather | solution.py:84
  467.4 4.6 bitcast_reduce_fusion
  472.2 161.6 %all-reduce.8.cloned.1.call-done = (f32[24,384]{0,1:T(8,128)}, f32[24,384]{0,1:T(8,128)}) async-done(((f32[24,384]{0,1:T(8,128)}, f32[24,384]{0,1:T(8,128)}), (f32[24,384]{0,1:T(8,128)}, f32[24,384]{0,1:T(8,128)})) %all-reduce.8.cloned.1.call-update) | async-done | bytes 73744 | tf_op jit(solution)/shard_map/psum | solution.py:142
  (239 shorter events, 276.3 us)
Async XLA Ops:
  40.1 5.9 collective-permute-start
  44.5 4.8 collective-permute-start.1
  85.1 18.2 %copy-start.22 = (s32[384,8]{0,1:T(8,128)S(1)}, s32[384,8]{0,1:T(8,128)}, u32[]{:S(2)}) copy-start(s32[384,8]{0,1:T(8,128)} %param.24) | copy-start | bytes 36868
  85.1 19.1 %copy-start.24 = (s32[384]{0:T(512)S(1)}, s32[384]{0:T(512)}, u32[]{:S(2)}) copy-start(s32[384]{0:T(512)} %param.25) | copy-start | bytes 4612
  87.8 18.4 %collective-permute-start.2 = (bf16[6,2,64,1,512]{4,2,3,1,0:T(8,128)(2,1)}, bf16[6,2,64,1,512]{4,2,3,1,0:T(8,128)(2,1)S(1)}, u32[]{:S(2)}, u32[]{:S(2)}) collective-permute-start(bf16[6,2,64,1,512]{4,2,3,1,0:T(8,128)(2,1)} %get-tuple-element.220), channel_id=1, source_target_pairs={{0,1},{1,2},{2,3},{3,4},{4,5},{5,6},{6,7},{7,8},{8,9},{9,10},{10,1... | collective-permute-start | bytes 2359304 | tf_op jit(solution)/shard_map/ppermute | solution.py:22
  91.2 18.8 %collective-permute-start.3 = (bf16[6,2,64,1,512]{4,2,3,1,0:T(8,128)(2,1)}, bf16[6,2,64,1,512]{4,2,3,1,0:T(8,128)(2,1)S(1)}, u32[]{:S(2)}, u32[]{:S(2)}) collective-permute-start(bf16[6,2,64,1,512]{4,2,3,1,0:T(8,128)(2,1)} %get-tuple-element.221), channel_id=1, source_target_pairs={{1,0},{2,1},{3,2},{4,3},{5,4},{6,5},{7,6},{8,7},{9,8},{10,9},{11,1... | collective-permute-start | bytes 2359304 | tf_op jit(solution)/shard_map/ppermute | solution.py:24
  93.6 292.5 %collective-permute-start.7 = (f32[24,2,16,1]{3,2,1,0:T(8,128)}, f32[24,2,16,1]{3,2,1,0:T(8,128)}, u32[]{:S(2)}, u32[]{:S(2)}) collective-permute-start(f32[24,2,16,1]{3,2,1,0:T(8,128)} %broadcast_in_dim.48), channel_id=1, source_target_pairs={{0,32},{32,64},{64,96},{1,33},{33,65},{65,97},{2,34},{34,66},{66,9... | collective-permute-start | bytes 9224 | tf_op jit(solution)/shard_map/ppermute | solution.py:22
  101.3 284.8 %collective-permute-start.8 = (f32[24,2,16,1]{3,2,1,0:T(8,128)}, f32[24,2,16,1]{3,2,1,0:T(8,128)}, u32[]{:S(2)}, u32[]{:S(2)}) collective-permute-start(f32[24,2,16,1]{3,2,1,0:T(8,128)} %broadcast_in_dim.50), channel_id=1, source_target_pairs={{32,0},{64,32},{96,64},{33,1},{65,33},{97,65},{34,2},{66,34},{98,6... | collective-permute-start | bytes 9224 | tf_op jit(solution)/shard_map/ppermute | solution.py:24
  105.0 15.3 %copy-start.20 = (bf16[64]{0:T(256)(128)(2,1)S(1)}, bf16[64]{0:T(256)(128)(2,1)}, u32[]{:S(2)}) copy-start(bf16[64]{0:T(256)(128)(2,1)} %param.21) | copy-start | bytes 388
  352.0 15.7 %all-to-all-start = ((f32[4,1,24576]{2,1,0:T(1,128)}), f32[4,1,24576]{2,1,0:T(1,128)S(1)}, u32[]{:S(2)}, u32[]{:S(2)}) async-start(f32[4,1,24576]{2,1,0:T(1,128)} %reshape.341), calls=%async_computation | async-start | bytes 786432 | tf_op jit(solution)/shard_map/all_to_all | solution.py:118
  359.6 274.3 %all-reduce.8.cloned.1.call-start = ((), (), s32[]{:S(2)}) async-start(), calls=%async_computation.1 | async-start | bytes 786432 | tf_op jit(solution)/shard_map/psum | solution.py:142
  381.4 11.5 %collective-permute-start.4 = (f32[24,2,16,1]{3,2,1,0:T(8,128)S(1)}, f32[24,2,16,1]{3,2,1,0:T(8,128)S(1)}, u32[]{:S(2)}, u32[]{:S(2)}) collective-permute-start(f32[24,2,16,1]{3,2,1,0:T(8,128)S(1)} %get-tuple-element.232), channel_id=1, source_target_pairs={{0,32},{32,64},{64,96},{1,33},{33,65},{65,97},{2,34},{34,66},{66,9... | collective-permute-start | bytes 9224 | tf_op jit(solution)/shard_map/ppermute | solution.py:22
  384.2 10.6 %collective-permute-start.5 = (f32[24,2,16,1]{3,2,1,0:T(8,128)S(1)}, f32[24,2,16,1]{3,2,1,0:T(8,128)S(1)}, u32[]{:S(2)}, u32[]{:S(2)}) collective-permute-start(f32[24,2,16,1]{3,2,1,0:T(8,128)S(1)} %get-tuple-element.233), channel_id=1, source_target_pairs={{32,0},{64,32},{96,64},{33,1},{65,33},{97,65},{34,2},{66,34},{98,6... | collective-permute-start | bytes 9224 | tf_op jit(solution)/shard_map/ppermute | solution.py:24
  387.8 12.5 %collective-permute-start.11 = (f32[24,2,1,130]{3,2,1,0:T(1,128)S(1)}, f32[24,2,1,130]{3,2,1,0:T(1,128)S(1)}, u32[]{:S(2)}, u32[]{:S(2)}) collective-permute-start(f32[24,2,1,130]{3,2,1,0:T(1,128)S(1)} %get-tuple-element.226), channel_id=1, source_target_pairs={{0,1},{1,2},{2,3},{3,4},{4,5},{5,6},{6,7},{7,8},{8,9},{9,10},{10,1... | collective-permute-start | bytes 74888 | tf_op jit(solution)/shard_map/ppermute | solution.py:22
  391.6 8.7 %collective-permute-start.9 = (f32[24,2,1,130]{3,2,1,0:T(1,128)S(1)}, f32[24,2,1,130]{3,2,1,0:T(1,128)S(1)}, u32[]{:S(2)}, u32[]{:S(2)}) collective-permute-start(f32[24,2,1,130]{3,2,1,0:T(1,128)S(1)} %get-tuple-element.227), channel_id=1, source_target_pairs={{1,0},{2,1},{3,2},{4,3},{5,4},{6,5},{7,6},{8,7},{9,8},{10,9},{11,1... | collective-permute-start | bytes 74888 | tf_op jit(solution)/shard_map/ppermute | solution.py:24
  395.2 6.9 %collective-permute-start.10 = (f32[24,2,1,130]{3,2,1,0:T(1,128)S(1)}, f32[24,2,1,130]{3,2,1,0:T(1,128)S(1)}, u32[]{:S(2)}, u32[]{:S(2)}) collective-permute-start(f32[24,2,1,130]{3,2,1,0:T(1,128)S(1)} %get-tuple-element.224), channel_id=1, source_target_pairs={{0,1},{1,2},{2,3},{3,4},{4,5},{5,6},{6,7},{7,8},{8,9},{9,10},{10,1... | collective-permute-start | bytes 74888 | tf_op jit(solution)/shard_map/ppermute | solution.py:22
  399.0 4.9 collective-permute-start.6
  409.3 22.3 %copy-start.25 = (f32[384]{0:T(512)S(1)}, f32[384]{0:T(512)}, u32[]{:S(2)}) copy-start(f32[384]{0:T(512)} %param.27) | copy-start | bytes 4612
  409.3 22.3 %copy-start.13 = (f32[6,256]{1,0:T(8,128)S(1)}, f32[6,256]{1,0:T(8,128)}, u32[]{:S(2)}) copy-start(f32[6,256]{1,0:T(8,128)} %param.17) | copy-start | bytes 18436
  409.5 10.3 %collective-permute-start.12 = (f32[24,2,16,1]{3,2,1,0:T(8,128)S(1)}, f32[24,2,16,1]{3,2,1,0:T(8,128)S(1)}, u32[]{:S(2)}, u32[]{:S(2)}) collective-permute-start(f32[24,2,16,1]{3,2,1,0:T(8,128)S(1)} %get-tuple-element.230), channel_id=1, source_target_pairs={{0,32},{32,64},{64,96},{1,33},{33,65},{65,97},{2,34},{34,66},{66,9... | collective-permute-start | bytes 9224 | tf_op jit(solution)/shard_map/ppermute | solution.py:22
  415.1 10.6 %collective-permute-start.13 = (f32[24,2,16,1]{3,2,1,0:T(8,128)S(1)}, f32[24,2,16,1]{3,2,1,0:T(8,128)S(1)}, u32[]{:S(2)}, u32[]{:S(2)}) collective-permute-start(f32[24,2,16,1]{3,2,1,0:T(8,128)S(1)} %get-tuple-element.231), channel_id=1, source_target_pairs={{32,0},{64,32},{96,64},{33,1},{65,33},{97,65},{34,2},{66,34},{98,6... | collective-permute-start | bytes 9224 | tf_op jit(solution)/shard_map/ppermute | solution.py:24
  419.8 17.7 %copy-start.4 = (f32[24,2,16,1]{3,2,1,0:T(8,128)}, f32[24,2,16,1]{3,2,1,0:T(8,128)S(1)}, u32[]{:S(2)}) copy-start(f32[24,2,16,1]{3,2,1,0:T(8,128)S(1)} %collective-permute-done.12) | copy-start | bytes 9220
  426.1 24.8 %collective-permute-start.14 = (f32[24,2,1,130]{3,2,1,0:T(1,128)S(1)}, f32[24,2,1,130]{3,2,1,0:T(1,128)S(1)}, u32[]{:S(2)}, u32[]{:S(2)}) collective-permute-start(f32[24,2,1,130]{3,2,1,0:T(1,128)S(1)} %get-tuple-element.223), channel_id=1, source_target_pairs={{1,0},{2,1},{3,2},{4,3},{5,4},{6,5},{7,6},{8,7},{9,8},{10,9},{11,1... | collective-permute-start | bytes 74888 | tf_op jit(solution)/shard_map/ppermute | solution.py:24
  427.4 23.5 %collective-permute-start.15 = (f32[24,2,1,130]{3,2,1,0:T(1,128)S(1)}, f32[24,2,1,130]{3,2,1,0:T(1,128)S(1)}, u32[]{:S(2)}, u32[]{:S(2)}) collective-permute-start(f32[24,2,1,130]{3,2,1,0:T(1,128)S(1)} %get-tuple-element.222), channel_id=1, source_target_pairs={{0,1},{1,2},{2,3},{3,4},{4,5},{5,6},{6,7},{7,8},{8,9},{9,10},{10,1... | collective-permute-start | bytes 74888 | tf_op jit(solution)/shard_map/ppermute | solution.py:22
  (20 other events, 174.6 us)
Sparse Core Ops, SparseCore 0:
  472.2 161.6 all-reduce.7
where the time goes:
time: 660 us; the launch traced here: 651 us
  matrix products  221 us (33%)
  waiting for transfers between devices  188 us (28%)
  local copies, waits for them, and re-layouts  107 us (16%)
  other arithmetic  58.8 us (9%)
  starting transfers between devices  55.2 us (8%)
  between operations  15.1 us (2%)
    psum x1, waiting for transfers between devices, body(): numer, weight_sum = lax.psum((numer, weight_sum), ('mem', 'tile'))  162 us
    dot_general x48, matrix products, mix(): jnp.einsum('oc,zcxy->zoxy', conv_mid[tap], part, preferred_element_type=j...  132 us
    dot_general x6, matrix products, mix(): return field + jnp.einsum('c,zcxy->zxy', conv_out.astype(jnp.float32), deep)  80.6 us
    ppermute x8, starting transfers between devices, extended(): lax.ppermute(tail, axis, [(i, (i + 1) % count) for i in range(ends)])  35 us
    unnamed x59, local copies, waits for them, and re-layouts  25.7 us
    convert_element_type x6, other arithmetic, lift(): return jax.nn.relu(total).astype(jnp.bfloat16)  18.8 us
    concatenate x8, other arithmetic, extended(): jnp.concatenate([lax.ppermute(tail, axis, [(i, (i + 1) % count) for i in...  17 us
    ppermute x8, waiting for transfers between devices, extended(): lax.ppermute(head, axis, [((i + 1) % count, i) for i in range(ends)])  16.6 us
  transfers between devices with their start and end apart: 18, of which 9 were waited for; matrix products, arithmetic and copies ran while one was open for 43% of the time, Pallas kernels for 0%

commit v1 on v0

v1 whole, which is shorter than its diff:
```python
import math

import jax
import jax.numpy as jnp
from jax import lax
from jax.experimental import pallas as pl
from jax.experimental.pallas import tpu as pltpu
from jax.sharding import PartitionSpec as P

SWEEPS = 2
STORAGE = 1.0
BF = jnp.bfloat16
F32 = jnp.float32
LANES = 128
HALO = 4
WINDOW = 32
PER_WINDOW = (WINDOW - 2) // 2
MESH = pl.DeviceIdType.MESH
BIG = 60 * 2**20


def dot(a, b):
    return jnp.dot(a, b, preferred_element_type=F32)


def dot_nt(a, b, precision=None):
    return lax.dot_general(a, b, (((1,), (1,)), ((), ())), preferred_element_type=F32, precision=precision)


def iota(shape, axis):
    return lax.broadcasted_iota(jnp.int32, shape, axis)


def ones_where(cond):
    return jnp.where(cond, 1.0, 0.0)


def field_kernel(
    lat_ref, basis_ref, prev_ref, source_ref, own_ref, halo_ref, edge_ref, every_ref,
    gathered, slab, left, send, edge_send, lat_sems, row_sems, slab_sems,
):
    mem = lax.axis_index("mem")
    tile = lax.axis_index("tile")
    mems = lax.axis_size("mem")
    tiles = lax.axis_size("tile")
    share, latent = lat_ref.shape
    members = share * mems
    rows = own_ref.shape[0]
    layers = basis_ref.shape[1]
    before, after = lax.rem(tile + tiles - 1, tiles), lax.rem(tile + 1, tiles)

    loads = []
    for part, offset in enumerate((0, -1, 1)):
        at = jnp.clip(mem + offset, 0, mems - 1)
        loads.append(
            pltpu.make_async_copy(
                basis_ref.at[:, :, :, pl.ds(pl.multiple_of(at * LANES, LANES), LANES)],
                slab.at[part],
                slab_sems.at[part],
            )
        )
    for load in loads:
        load.start()

    barrier = pltpu.get_barrier_semaphore()
    for step in range(1, mems):
        pl.semaphore_signal(barrier, inc=1, device_id={"mem": lax.rem(mem + step, mems)}, device_id_type=MESH)
    for other in (before, after):
        pl.semaphore_signal(barrier, inc=1, device_id={"tile": other}, device_id_type=MESH)
    pl.semaphore_wait(barrier, mems + 1)

    copies = []
    for step in range(1, mems):
        copies.append(
            pltpu.make_async_remote_copy(
                src_ref=lat_ref,
                dst_ref=gathered.at[mem],
                send_sem=lat_sems.at[0, step],
                recv_sem=lat_sems.at[1, step],
                device_id={"mem": lax.rem(mem + step, mems)},
                device_id_type=MESH,
            )
        )
        copies[-1].start()

    for side in range(2):
        first = 0 if side == 0 else rows - 2
        edge = 0 if side == 0 else rows - 1
        for z in range(layers):
            edge_send[side, 2 * z : 2 * z + 2] = prev_ref[z, first : first + 2]
            edge_send[side, 4 + z : 5 + z] = source_ref[z, edge : edge + 1]
        edge_send[side, 6:8] = jnp.zeros_like(edge_send[side, 6:8])
    row_copies = []
    for side, other in ((0, before), (1, after)):
        row_copies.append(
            pltpu.make_async_remote_copy(
                src_ref=edge_send.at[side],
                dst_ref=edge_ref.at[1 - side],
                send_sem=row_sems.at[0, side],
                recv_sem=row_sems.at[1, side],
                device_id={"tile": other},
                device_id_type=MESH,
            )
        )
        row_copies[-1].start()

    gathered[mem] = lat_ref[...]
    for copy in copies:
        copy.wait()
    for s in range(mems):
        every_ref[share * s : share * (s + 1)] = gathered[s]
    every = every_ref[...].astype(BF).astype(F32)

    groups = latent // rows
    wide = rows * rows
    group_of = iota((1, latent), 1) // rows
    picked = jnp.concatenate([every * ones_where(group_of == g) for g in range(groups)], axis=0).astype(BF)
    spread = ones_where(lax.rem(iota((latent, wide), 0), rows) == iota((latent, wide), 1) // rows).astype(BF)
    repeated = dot(picked, spread)
    lane_row = lax.rem(iota((1, wide), 1), rows)
    for g in range(groups):
        part = repeated[g * members : (g + 1) * members]
        stacked = jnp.concatenate([part * ones_where(lane_row == r) for r in range(rows)], axis=0)
        left[:, g * wide : (g + 1) * wide] = stacked.astype(BF)
    for load in loads:
        load.wait()
    lane = iota((1, LANES), 1)
    keep_left = (ones_where(lane >= LANES // 2) * jnp.where(mem > 0, 1.0, 0.0)).astype(BF)
    keep_right = (ones_where(lane < LANES // 2) * jnp.where(mem < mems - 1, 1.0, 0.0)).astype(BF)
    for z in range(layers):
        own = slab[0, :, z].reshape(latent * rows, LANES)
        lhs = slab[1, :, z].reshape(latent * rows, LANES)
        rhs = slab[2, :, z].reshape(latent * rows, LANES)
        both = jnp.concatenate([own, lhs * keep_left + rhs * keep_right], axis=1)
        field = dot(left[...], both).reshape(rows, members, 2 * LANES)
        own_ref[:, z * members : (z + 1) * members] = field
    send[0:HALO] = own_ref[0:HALO].astype(BF)
    send[HALO : 2 * HALO] = own_ref[rows - HALO : rows].astype(BF)
    for side, other in ((0, before), (1, after)):
        row_copies.append(
            pltpu.make_async_remote_copy(
                src_ref=send.at[pl.ds(side * HALO, HALO)],
                dst_ref=halo_ref.at[pl.ds((1 - side) * HALO, HALO)],
                send_sem=row_sems.at[0, 2 + side],
                recv_sem=row_sems.at[1, 2 + side],
                device_id={"tile": other},
                device_id_type=MESH,
            )
        )
        row_copies[-1].start()
    for copy in row_copies:
        copy.wait()


def fields(latents, basis, prev, source):
    share, latent = latents.shape
    mems = lax.axis_size("mem")
    members = share * mems
    _, layers, rows, width = basis.shape
    vmem = pl.BlockSpec(memory_space=pltpu.VMEM)
    return pl.pallas_call(
        field_kernel,
        out_shape=[
            jax.ShapeDtypeStruct((rows, layers * members, 2 * LANES), F32),
            jax.ShapeDtypeStruct((2 * HALO, layers * members, 2 * LANES), BF),
            jax.ShapeDtypeStruct((2, 8, width), F32),
            jax.ShapeDtypeStruct((members, latent), F32),
        ],
        in_specs=[vmem, pl.BlockSpec(memory_space=pl.ANY), vmem, vmem],
        out_specs=[vmem] * 4,
        scratch_shapes=[
            pltpu.VMEM((mems, share, latent), F32),
            pltpu.VMEM((3, latent, layers, rows, LANES), BF),
            pltpu.VMEM((rows * members, latent * rows), BF),
            pltpu.VMEM((2 * HALO, layers * members, 2 * LANES), BF),
            pltpu.VMEM((2, 8, width), F32),
            pltpu.SemaphoreType.DMA((2, mems)),
            pltpu.SemaphoreType.DMA((2, 4)),
            pltpu.SemaphoreType.DMA((3,)),
        ],
        compiler_params=pltpu.CompilerParams(collective_id=0, has_side_effects=True, vmem_limit_bytes=BIG),
        name="fields",
    )(latents, basis, prev, source)


def decoder_weights(conv_in_ref, conv_mid_ref, conv_out_ref, taps, lift_w, mix_w, out_w, mem, mems, last):
    channels = conv_out_ref.shape[1]
    block = 4 * channels
    taps[...] = jnp.zeros_like(taps)
    taps[0:9] = conv_in_ref[...].astype(F32)
    repeat = ones_where(iota((channels, block), 0) == lax.rem(iota((channels, block), 1), channels)).astype(BF)
    in_rows = dot(taps[...].astype(BF), repeat)
    in_rows = jnp.concatenate([in_rows] * 4, axis=0)
    in_rows = (in_rows * ones_where(iota((64, block), 0) // 16 == iota((64, block), 1) // channels)).astype(BF)
    row = iota((block, 64), 0)
    col = iota((block, 64), 1)
    column = lax.rem(row, WINDOW)
    patch_row = lax.rem(row // WINDOW, 4)
    tap = lax.rem(col, 16)
    tap_row = jnp.where(tap >= 3, 1, 0) + jnp.where(tap >= 6, 1, 0)
    tap_col = tap - 3 * tap_row
    fits = (patch_row == col // 32 + tap_row) & (tap < 9)
    offset = jnp.where(fits, column - lax.rem(col // 16, 2) - tap_col, -1)
    col_of = lax.rem(iota((1, block), 1) // channels, 2)
    low, high = jnp.where(mem > 0, 1.0, 0.0), jnp.where(mem < mems - 1, 1.0, 0.0)
    for t in range(PER_WINDOW):
        weight = dot(ones_where(offset == 2 * t).astype(BF), in_rows)
        lift_w[t] = weight.astype(BF)
        if t == 0:
            lift_w[PER_WINDOW] = (weight * low).astype(BF)
        if t == 1:
            lift_w[PER_WINDOW + 1] = (weight * jnp.where(col_of == 0, low, 1.0)).astype(BF)
        if t == (last - 1) % PER_WINDOW:
            lift_w[PER_WINDOW + 2] = (weight * jnp.where(col_of == 1, high, 1.0)).astype(BF)
        if t == last % PER_WINDOW:
            lift_w[PER_WINDOW + 3] = (weight * high).astype(BF)
    mix_w[...] = jnp.zeros_like(mix_w)
    nothing = jnp.zeros((channels, channels), F32)
    for p in range(4):
        for q in range(4):
            at = ((q // 2) * 2 + p // 2) * block + ((p % 2) * 2 + q % 2) * channels
            for a in range(2):
                if not 0 <= p - a <= 2:
                    continue
                pair = [
                    conv_mid_ref[3 * (p - a) + q - b].astype(F32) if 0 <= q - b <= 2 else nothing for b in range(2)
                ]
                mix_w[at : at + channels, a * 2 * channels : (a + 1) * 2 * channels] = (
                    jnp.concatenate(pair, axis=0).T.astype(BF)
                )
    out_row = conv_out_ref[...].astype(F32)
    diag = iota((channels, channels), 0) == iota((channels, channels), 1)
    out_col = jnp.sum(jnp.where(diag, out_row, 0.0), axis=1, keepdims=True)
    out_col = jnp.concatenate([out_col] * 4, axis=0)
    group = iota((block, 2 * LANES), 0) // channels
    lane = iota((block, 2 * LANES), 1)
    match = (group // 2 == lane // LANES) & (lax.rem(group, 2) == lax.rem(lane, 2))
    out_w[...] = jnp.where(match, out_col, 0.0).astype(BF)


def field_windows(own_ref, halo_ref, windows, pieces, tile, tiles):
    rows = own_ref.shape[0]
    lane = iota((1, LANES), 1)
    top = jnp.where(tile > 0, 1.0, 0.0)
    bottom = jnp.where(tile < tiles - 1, 1.0, 0.0)
    count = windows.shape[0]

    def row_pieces(field, odd):
        own, halo = field[:, :LANES], field[:, LANES:]
        low = jnp.where(lane < LANES // 2, own, halo)
        high = jnp.where(lane < LANES // 2, halo, own)
        out = []
        for w in range(count):
            start = (WINDOW - 2) * w - HALO
            from_tile = low if w == 0 else high if w == count - 1 else own
            out.append(pltpu.roll(from_tile, (WINDOW * odd - start) % LANES, 1))
        return out

    def pair_pieces(q, even, odd):
        evens, odds = row_pieces(even, 0), row_pieces(odd, 1)
        for w in range(count):
            pieces[q, w] = jnp.where(lane < WINDOW, evens[w], odds[w])

    for half in range(HALO // 2):
        pair_pieces(half, halo_ref[2 * half].astype(F32) * top, halo_ref[2 * half + 1].astype(F32) * top)
        at = HALO + 2 * half
        pair_pieces(
            (rows + at) // 2, halo_ref[at].astype(F32) * bottom, halo_ref[at + 1].astype(F32) * bottom
        )

    def own_pair(q, carry):
        pair_pieces(q + HALO // 2, own_ref[2 * q], own_ref[2 * q + 1])
        return carry

    lax.fori_loop(0, rows // 2, own_pair, 0)
    members = own_ref.shape[1]

    def block_row(i, carry):
        for w in range(count):
            both = jnp.where(lane < LANES // 2, pieces[i, w], pltpu.roll(pieces[i + 1, w], LANES // 2, 1))
            high = both.astype(BF)
            windows[w, i] = jnp.concatenate([high, (both - high.astype(F32)).astype(BF)], axis=1)
        return carry

    lax.fori_loop(0, windows.shape[1], block_row, 0)


def convolve(windows, lift_w, mix_w, out_w, lifted, mixed, total, ends, tile, tiles, blocks):
    count, block_rows, deep, _ = windows.shape
    size = (block_rows - 1) * deep
    lane = iota((1, 2 * LANES), 1)
    pair = lax.rem(lane, LANES) // 2
    part = lane // LANES
    top = jnp.where(tile > 0, 1.0, 0.0)
    bottom = jnp.where(tile < tiles - 1, 1.0, 0.0)
    masks = {
        0: jnp.zeros((1, 2 * LANES), F32) + top,
        1: jnp.where(part == 0, top, 1.0),
        block_rows - 2: jnp.where(part == 1, bottom, 1.0),
        block_rows - 1: jnp.zeros((1, 2 * LANES), F32) + bottom,
    }

    def lift(k, slot):
        for u in range(2):
            at = jnp.minimum(2 * k + u, blocks)
            w = at // PER_WINDOW
            index = at - w * PER_WINDOW
            for special, j in enumerate((0, 1, blocks - 1, blocks)):
                index = jnp.where(at == j, PER_WINDOW + special, index)
            value = jnp.maximum(dot(windows[w].reshape(block_rows * deep, -1), lift_w[index]), 0.0)
            parts = [value[i * deep : (i + 1) * deep] for i in range(block_rows)]
            parts = [p * masks[i] if i in masks else p for i, p in enumerate(parts)]
            lifted[slot][u] = jnp.concatenate(parts, axis=0).astype(BF)

    def mix(k, slot, to):
        held = [lifted[slot].at[0], lifted[slot].at[1], lifted[(slot + 1) % 3].at[0]]
        for u in range(2):
            x, y = held[u], held[u + 1]
            lhs = jnp.concatenate([x[0:size], x[deep : deep + size], y[0:size], y[deep : deep + size]], axis=1)
            mixed[to][u] = jnp.maximum(dot(lhs, mix_w[...]), 0.0).astype(BF)

    def contract(k, at, first=False, last=False):
        even = dot(mixed[at][0], out_w[...])
        odd = dot(mixed[at][1], out_w[...])
        j = 2 * k
        if first:
            ends[...] = even
            total[...] = odd
        elif last:
            total[...] = jnp.where(pair == j - 1, even, total[...])
            ends[...] = jnp.where(pair == 0, odd, ends[...])
        else:
            total[...] = jnp.where(pair == j - 1, even, jnp.where(pair == j, odd, total[...]))

    steps = blocks // 2
    lift(0, 0)
    lift(1, 1)
    mix(0, 0, 0)
    lift(2, 2)
    contract(0, 0, first=True)
    mix(1, 1, 1)
    lift(3, 0)

    def body(q, carry):
        for v in range(6):
            k = 2 + q * 6 + v
            contract(k - 1, (1 + v) % 2)
            mix(k, (2 + v) % 3, v % 2)
            lift(k + 2, (4 + v) % 3)
        return carry

    lax.fori_loop(0, (steps - 3) // 6, body, 0)
    k = steps - 1
    contract(k - 1, (k - 1) % 2)
    mix(k, k % 3, k % 2)
    contract(k, k % 2, last=True)


def sweeps(
    own_ref, halo_ref, edge_ref, prev_ref, source_ref, total, ends, perm, first, press_ref, values,
    mem, mems, tile, tiles,
):
    rows = own_ref.shape[0]
    deep = own_ref.shape[1]
    layers = prev_ref.shape[0]
    members = deep // layers
    lane = iota((1, LANES), 1)
    top = jnp.where(tile > 0, 1.0, 0.0)
    bottom = jnp.where(tile < tiles - 1, 1.0, 0.0)
    beyond = jnp.where(lane < LANES // 2, jnp.where(mem < mems - 1, 1.0, 0.0), jnp.where(mem > 0, 1.0, 0.0))
    mine = pl.multiple_of(mem * LANES, LANES)
    before = pl.multiple_of(jnp.maximum(mem - 1, 0) * LANES, LANES)
    after = pl.multiple_of(jnp.minimum(mem + 1, mems - 1) * LANES, LANES)

    def columns(line):
        beside = jnp.where(lane < LANES // 2, line(after), line(before))
        return line(mine), beside

    def levels(pick):
        each = [columns(lambda at: pick(z, at)) for z in range(layers)]
        return [
            jnp.concatenate([jnp.broadcast_to(each[z][t], (members, LANES)) for z in range(layers)], axis=0)
            for t in range(2)
        ]

    def prev_line(index):
        r = index - 2
        if r < 0:
            return levels(lambda z, at: edge_ref[0, 2 * z + 2 + r : 2 * z + 3 + r, pl.ds(at, LANES)])
        if r >= rows:
            return levels(lambda z, at: edge_ref[1, 2 * z + r - rows : 2 * z + r - rows + 1, pl.ds(at, LANES)])
        return levels(lambda z, at: prev_ref[z, r : r + 1, pl.ds(at, LANES)])

    def source_line(index):
        r = index - 2
        if r < 0:
            return levels(lambda z, at: edge_ref[0, 4 + z : 5 + z, pl.ds(at, LANES)])
        if r >= rows:
            return levels(lambda z, at: edge_ref[1, 4 + z : 5 + z, pl.ds(at, LANES)])
        return levels(lambda z, at: source_ref[z, r : r + 1, pl.ds(at, LANES)])

    for index in range(rows + 4):
        r = index - 2
        i, a = index // 2, index % 2
        for t, parts in enumerate((total, ends)):
            value = parts[i * deep : (i + 1) * deep, a * LANES : (a + 1) * LANES]
            if 0 <= r < rows:
                field = own_ref[r, :, t * LANES : (t + 1) * LANES]
            else:
                at = HALO + r if r < 0 else HALO + r - rows
                field = halo_ref[at, :, t * LANES : (t + 1) * LANES].astype(F32)
            value = jnp.exp(field + value)
            if r < 0:
                value = jnp.where(top > 0, value, 0.0)
            if r >= rows:
                value = jnp.where(bottom > 0, value, 0.0)
            if t == 1:
                value = jnp.where(beyond > 0, value, 0.0)
            perm[index, t] = value

    def shift(own, beside, by):
        edge = LANES - 1 if by > 0 else 0
        a, b = pltpu.roll(own, -by % LANES, 1), pltpu.roll(beside, -by % LANES, 1)
        return jnp.where(lane == edge, b, a), jnp.where(lane == edge, a, b)

    def harmonic(a, b):
        both = a + b
        return jnp.where(both > 0, 2.0 * a * b / jnp.where(both > 0, both, 1.0), 0.0)

    def swap(x):
        return jnp.concatenate([x[members:], x[:members]], axis=0)

    def coefficients(index):
        here = [perm[index, t] for t in range(2)]
        right = shift(here[0], here[1], 1)
        across = [harmonic(here[t], right[t]) for t in range(2)]
        back = shift(across[0], across[1], -1)
        out = []
        for t in range(2):
            level = harmonic(here[t][:members], here[t][members:])
            out.append((across[t], back[t], jnp.concatenate([level, level], axis=0)))
        return out

    up = [harmonic(perm[0, t], perm[1, t]) for t in range(2)]
    lines = [prev_line(0), prev_line(1)]
    for index in range(1, rows + 3):
        lines.append(prev_line(index + 1))
        down = [harmonic(perm[index, t], perm[index + 1, t]) for t in range(2)]
        coef = coefficients(index)
        here = lines[index]
        right, back = shift(here[0], here[1], 1), shift(here[0], here[1], -1)
        source = source_line(index)
        for t in range(2):
            east, west, level = coef[t]
            acc = STORAGE * here[t] + source[t]
            acc = acc + down[t] * lines[index + 1][t] + up[t] * lines[index - 1][t]
            acc = acc + east * right[t] + west * back[t] + level * swap(here[t])
            first[index, t] = acc / (STORAGE + down[t] + up[t] + east + west + level)
        up = down
    up = harmonic(perm[1, 0], perm[2, 0])
    for index in range(2, rows + 2):
        r = index - 2
        down = harmonic(perm[index, 0], perm[index + 1, 0])
        east, west, level = coefficients(index)[0]
        here = first[index, 0]
        right = shift(here, first[index, 1], 1)[0]
        back = shift(here, first[index, 1], -1)[0]
        acc = STORAGE * lines[index][0] + source_line(index)[0]
        acc = acc + down * first[index + 1, 0] + up * first[index - 1, 0]
        acc = acc + east * right + west * back + level * swap(here)
        press = acc / (STORAGE + down + up + east + west + level)
        up = down
        k = perm[index, 0]
        for z in range(layers):
            level_press = press[z * members : (z + 1) * members]
            level_perm = k[z * members : (z + 1) * members]
            press_ref[:, z, r, :] = level_press
            at = (z * rows + r) * LANES
            for q, value in enumerate((level_perm, level_perm * level_press)):
                high = value.astype(BF).astype(F32)
                both = jnp.concatenate([high, value - high], axis=0).astype(BF)
                values[2 * q * members : 2 * (q + 1) * members, at : at + LANES] = both


def well_sums(cells_ref, count_ref, values, pick, pieces_ref, mem, tile, grid_cols, grid_cells, rows):
    wells, slots = cells_ref.shape
    groups, members, _ = pieces_ref.shape
    each = wells // groups
    cells = cells_ref[...]
    layer = cells // grid_cells
    rest = cells - layer * grid_cells
    row = rest // grid_cols
    col = rest - row * grid_cols - mem * LANES
    row = row - tile * rows
    square = (iota((wells, wells), 0), iota((wells, wells), 1))
    counts = jnp.sum(jnp.where(square[0] == square[1], count_ref[...].astype(F32), 0.0), axis=1, keepdims=True)
    used = iota((wells, slots), 1).astype(F32) < counts
    inside = (row >= 0) & (row < rows) & (col >= 0) & (col < LANES) & used
    mask = ones_where(inside)
    code = (((layer * rows + row) * LANES + col) * 512 + iota((wells, slots), 0) + 1).astype(F32)
    code = jnp.where(inside, code, 0.0)
    earlier = dot(ones_where(square[1] < square[0]).astype(BF), mask.astype(BF))
    totals = jnp.sum(mask, axis=0, keepdims=True)
    rank = []
    start = jnp.zeros((1, 1), F32)
    for s in range(slots):
        rank.append(jnp.where(inside[:, s : s + 1], earlier[:, s : s + 1] + start, -1.0))
        start = start + totals[:, s : s + 1]
    code = [code[:, s : s + 1] for s in range(slots)]
    chunks = (jnp.sum(mask).astype(jnp.int32) + LANES - 1) // LANES
    pieces_ref[...] = jnp.zeros_like(pieces_ref)
    cells_local = values.shape[1]
    place = lax.rem(iota((groups * LANES, LANES), 0), LANES)
    well_at = iota((groups * LANES, LANES), 0) // LANES * each + place
    number = jnp.where(place < each, well_at, -7)
    weight = jnp.where((place >= each) & (place < 2 * each), well_at - each, -7)

    def chunk(n, carry):
        wanted = (iota((1, LANES), 1) + n * LANES).astype(F32)
        found = jnp.zeros((1, LANES), F32)
        for s in range(slots):
            found = found + jnp.sum(jnp.where(rank[s] == wanted, code[s], 0.0), axis=0, keepdims=True)
        found = found.astype(jnp.int32) - 1
        cell = jnp.where(found >= 0, found // 512, -1)
        well = jnp.where(found >= 0, lax.rem(found, 512), -1)
        pick[...] = ones_where(iota((cells_local, LANES), 0) == cell).astype(BF)
        got = dot(values[...], pick[...])
        for q, (target, name) in enumerate(((weight, "w"), (number, "n"))):
            sums = got[2 * q * members : (2 * q + 1) * members] + got[(2 * q + 1) * members : (2 * q + 2) * members]
            high = sums.astype(BF).astype(F32)
            both = jnp.concatenate([high, sums - high], axis=0).astype(BF)
            out = dot_nt(both, ones_where(target == well).astype(BF))
            out = out[:members] + out[members:]
            for g in range(groups):
                pieces_ref[g] += out[:, g * LANES : (g + 1) * LANES]
        return carry

    lax.fori_loop(0, chunks, chunk, 0)


def cells_kernel(
    own_ref, halo_ref, edge_ref, conv_in_ref, conv_mid_ref, conv_out_ref, prev_ref, source_ref, cells_ref, count_ref,
    press_ref, pieces_ref,
    taps, lift_w, mix_w, out_w, pieces, windows, l0, l1, l2, m0, m1, total, ends, perm, first, values, pick,
):
    mem, mems = lax.axis_index("mem"), lax.axis_size("mem")
    tile, tiles = lax.axis_index("tile"), lax.axis_size("tile")
    rows = own_ref.shape[0]
    blocks = LANES // 2 + 2
    decoder_weights(conv_in_ref, conv_mid_ref, conv_out_ref, taps, lift_w, mix_w, out_w, mem, mems, blocks)
    field_windows(own_ref, halo_ref, windows, pieces, tile, tiles)
    convolve(windows, lift_w, mix_w, out_w, (l0, l1, l2), (m0, m1), total, ends, tile, tiles, blocks)
    sweeps(
        own_ref, halo_ref, edge_ref, prev_ref, source_ref, total, ends, perm, first, press_ref, values,
        mem, mems, tile, tiles,
    )
    grid_cols = prev_ref.shape[2]
    well_sums(
        cells_ref, count_ref, values, pick, pieces_ref, mem, tile, grid_cols, grid_cols * rows * tiles, rows
    )


def cells(own, halo, edge, conv_in, conv_mid, conv_out, prev, source, perf_cells, perf_count, groups):
    rows, deep, _ = own.shape
    layers = prev.shape[0]
    members = deep // layers
    channels = conv_in.shape[1]
    block = 4 * channels
    blocks = LANES // 2 + 2
    count = blocks // PER_WINDOW + 1
    out_rows = rows // 2 + 2
    vmem = pl.BlockSpec(memory_space=pltpu.VMEM)
    return pl.pallas_call(
        cells_kernel,
        out_shape=[
            jax.ShapeDtypeStruct((members, layers, rows, LANES), F32),
            jax.ShapeDtypeStruct((groups, members, LANES), F32),
        ],
        in_specs=[vmem] * 10,
        out_specs=[vmem] * 2,
        scratch_shapes=[
            pltpu.VMEM((16, channels), F32),
            pltpu.VMEM((PER_WINDOW + 4, block, block), BF),
            pltpu.VMEM((4 * block, block), BF),
            pltpu.VMEM((block, 2 * LANES), BF),
            pltpu.VMEM((rows // 2 + HALO, count, deep, LANES), F32),
            pltpu.VMEM((count, out_rows + 1, deep, 2 * LANES), BF),
        ]
        + [pltpu.VMEM((2, (out_rows + 1) * deep, block), BF)] * 3
        + [pltpu.VMEM((2, out_rows * deep, block), BF)] * 2
        + [pltpu.VMEM((out_rows * deep, 2 * LANES), F32)] * 2
        + [pltpu.VMEM((rows + 4, 2, deep, LANES), F32)] * 2
        + [
            pltpu.VMEM((4 * members, layers * rows * LANES), BF),
            pltpu.VMEM((layers * rows * LANES, LANES), BF),
        ],
        compiler_params=pltpu.CompilerParams(vmem_limit_bytes=BIG),
        name="cells",
    )(own, halo, edge, conv_in, conv_mid, conv_out.reshape(1, channels), prev, source, perf_cells,
      perf_count.reshape(1, -1))


def smoother_kernel(
    pieces_ref, every_ref, obs_ref, error_ref, well_ref, new_ref,
    group_in, y_in, z_in, data_in, hold, group_sems, y_sems, z_sems, data_sems,
):
    mem, tile = lax.axis_index("mem"), lax.axis_index("tile")
    mems = lax.axis_size("mem")
    side = y_in.shape[0]
    plane = side * side
    halves = lax.axis_size("tile") // plane
    groups = mems * halves
    x_lo, y, z = tile // plane, lax.rem(tile // side, side), lax.rem(tile, side)
    mine = mem * halves + x_lo
    members = every_ref.shape[0]

    def in_group(g):
        return {"mem": g // halves, "tile": lax.rem(g, halves) * plane + lax.rem(tile, plane)}

    def along_y(at):
        return {"mem": mem, "tile": x_lo * plane + at * side + z}

    def along_z(at):
        return {"mem": mem, "tile": x_lo * plane + y * side + at}

    barrier = pltpu.get_barrier_semaphore()
    for place, at, size in ((in_group, mine, groups), (along_y, y, side), (along_z, z, side)):
        for step in range(1, size):
            pl.semaphore_signal(barrier, inc=1, device_id=place(lax.rem(at + step, size)), device_id_type=MESH)
    pl.semaphore_wait(barrier, groups + 2 * side - 3)

    def exchange(place, at, size, source, target, sems):
        copies = []
        for step in range(1, size):
            to = lax.rem(at + step, size)
            copies.append(
                pltpu.make_async_remote_copy(
                    src_ref=source(to),
                    dst_ref=target.at[at],
                    send_sem=sems.at[0, step],
                    recv_sem=sems.at[1, step],
                    device_id=place(to),
                    device_id_type=MESH,
                )
            )
            copies[-1].start()
        return copies

    def total(target, size):
        value = target[0]
        for at in range(1, size):
            value = value + target[at]
        return value

    copies = exchange(in_group, mine, groups, lambda to: pieces_ref.at[to], group_in, group_sems)
    group_in[mine] = pieces_ref[mine]
    for copy in copies:
        copy.wait()
    for stage, (place, at, target, sems, source) in enumerate(
        ((along_y, y, y_in, y_sems, group_in), (along_z, z, z_in, z_sems, y_in))
    ):
        value = total(source, source.shape[0])
        hold[stage] = value
        target[at] = value
        copies = exchange(place, at, side, lambda to: hold.at[stage], target, sems)
        for copy in copies:
            copy.wait()
    value = total(z_in, side)
    each = obs_ref.shape[1] // groups
    data = value / pltpu.roll(value, LANES - each, 1)
    hold[2] = data
    data_in[mine] = data
    copies = exchange(in_group, mine, groups, lambda to: hold.at[2], data_in, data_sems)
    for copy in copies:
        copy.wait()

    lane = iota((1, LANES), 1)
    parts = []
    for t in range(obs_ref.shape[1] // LANES):
        part = jnp.zeros((members, LANES), F32)
        for g in range(groups):
            by = each * g - LANES * t
            if by <= -each or by >= LANES:
                continue
            moved = pltpu.roll(data_in[g], by % LANES, 1)
            part = jnp.where((lane >= by) & (lane < by + each), moved, part)
        parts.append(part)
    wells = jnp.concatenate(parts, axis=1)
    well_ref[...] = wells
    scale = 2.0 * error_ref[...]
    centred = wells - jnp.sum(wells, axis=0, keepdims=True) / members
    scaled = centred / (math.sqrt(members - 1) * scale)
    innov = (obs_ref[...] - wells) / scale
    exact = lax.Precision.HIGHEST
    eye = ones_where(iota((members, members), 0) == iota((members, members), 1))
    gram = eye + dot_nt(scaled, scaled, exact)
    cross = dot_nt(innov, scaled, exact)
    work = jnp.concatenate([gram, eye], axis=1)
    row_at = iota((members, 1), 0)
    for k in range(members):
        line = work[k : k + 1] / work[k : k + 1, k : k + 1]
        work = jnp.where(row_at == k, line, work - work[:, k : k + 1] * line)
    inverse = work[:, members:]
    weights = jnp.dot(cross, inverse, preferred_element_type=F32, precision=exact)
    every = every_ref[...]
    spread = (every - jnp.sum(every, axis=0, keepdims=True) / members) / math.sqrt(members - 1)
    new = every + jnp.dot(weights, spread, preferred_element_type=F32, precision=exact)
    share = members // mems
    own = new[0:share]
    for s in range(1, mems):
        own = jnp.where(mem == s, new[s * share : (s + 1) * share], own)
    new_ref[...] = own


def smooth(pieces, every, obs, error):
    groups, members, _ = pieces.shape
    mems, tiles = lax.axis_size("mem"), lax.axis_size("tile")
    side = math.isqrt(tiles * mems // groups)
    vmem = pl.BlockSpec(memory_space=pltpu.VMEM)
    return pl.pallas_call(
        smoother_kernel,
        out_shape=[
            jax.ShapeDtypeStruct(obs.shape, F32),
            jax.ShapeDtypeStruct((members // mems, every.shape[1]), F32),
        ],
        in_specs=[vmem] * 4,
        out_specs=[vmem] * 2,
        scratch_shapes=[
            pltpu.VMEM((groups, members, LANES), F32),
            pltpu.VMEM((side, members, LANES), F32),
            pltpu.VMEM((side, members, LANES), F32),
            pltpu.VMEM((groups, members, LANES), F32),
            pltpu.VMEM((3, members, LANES), F32),
            pltpu.SemaphoreType.DMA((2, groups)),
            pltpu.SemaphoreType.DMA((2, side)),
            pltpu.SemaphoreType.DMA((2, side)),
            pltpu.SemaphoreType.DMA((2, groups)),
        ],
        compiler_params=pltpu.CompilerParams(collective_id=1, has_side_effects=True, vmem_limit_bytes=BIG),
        name="smoother",
    )(pieces, every, obs, error.reshape(1, -1))


def body(
    latents, basis, conv_in, conv_mid, conv_out, pressure_prev, source, perf_cells, perf_count, obs_perturbed, obs_error
):
    groups = 2 * lax.axis_size("mem")
    own, halo, edge, every = fields(latents, basis, pressure_prev, source)
    press, pieces = cells(
        own, halo, edge, conv_in, conv_mid, conv_out, pressure_prev, source, perf_cells, perf_count, groups
    )
    well_data, latents_new = smooth(pieces, every, obs_perturbed, obs_error)
    return press, well_data, latents_new


def solution(mesh):
    return jax.shard_map(
        body,
        mesh=mesh,
        in_specs=(
            P("mem", None), P(None, None, "tile", None), P(), P(), P(), P(None, "tile", None), P(None, "tile", None),
            P(), P(), P(), P(),
        ),
        out_specs=(P(None, None, "tile", "mem"), P(), P("mem", None)),
        check_vma=False,
    )
```

time: 660 us -> 87.2 us (0.13); the launches traced: 651 us -> 86.9 us
  matrix products: 221 us -> 0 us
  waiting for transfers between devices: 188 us -> 0 us
  local copies, waits for them, and re-layouts: 107 us -> 4.64 us
  Pallas kernels: 0 us -> 81.6 us
  other arithmetic: 58.8 us -> 0 us
  starting transfers between devices: 55.2 us -> 0 us
  between operations: 15.1 us -> 0.68 us
    dot_general x58 -> x0, matrix products: 221 us -> none  [the longest x48 132 us: mix(): jnp.einsum('oc,zcxy->zoxy', conv_mid[tap], part, preferred_element_type=j...]
    psum x1 -> x0, waiting for transfers between devices: 162 us -> none  [body(): numer, weight_sum = lax.psum((numer, weight_sum), ('mem', 'tile'))]
    pallas_call x0 -> x3, Pallas kernels: none -> 81.6 us  [the longest x1 37.6 us: cells(): pl.pallas_call(cells_kernel, out_shape=[jax.ShapeDtypeStruct((members, la...]
    ppermute x16 -> x0, starting transfers between devices: 47.3 us -> none  [the longest x8 35 us: extended(): lax.ppermute(tail, axis, [(i, (i + 1) % count) for i in range(ends)])]
    unnamed x59 -> x9, local copies, waits for them, and re-layouts: 25.7 us -> 3.51 us
    gather x2 -> x0, local copies, waits for them, and re-layouts: 21.7 us -> none  [the longest x1 10.8 us: well_terms(): press_at = jnp.take(press.reshape(members, -1), local_ids, axis=1)]
    ppermute x16 -> x0, waiting for transfers between devices: 20.6 us -> none  [the longest x8 16.6 us: extended(): lax.ppermute(head, axis, [((i + 1) % count, i) for i in range(ends)])]
    convert_element_type x12 -> x0, other arithmetic: 18.8 us -> none  [the longest x6 18.8 us: lift(): return jax.nn.relu(total).astype(jnp.bfloat16)]
  transfers between devices with their start and end apart: 18 -> 0, of which waited for: 9 -> 0; matrix products, arithmetic and copies ran while one was open for 43% -> 0% of each run, Pallas kernels for 0% -> 0%
where the time goes in v1:
time: 87.2 us; the launch traced here: 86.9 us
  Pallas kernels  81.6 us (94%)
  local copies, waits for them, and re-layouts  4.64 us (5%)
    pallas_call x1, Pallas kernels, cells(): pl.pallas_call(cells_kernel, out_shape=[jax.ShapeDtypeStruct((members, la...  37.6 us
    pallas_call x1, Pallas kernels, smooth(): pl.pallas_call(smoother_kernel, out_shape=[jax.ShapeDtypeStruct(obs.shape...  23.2 us
    pallas_call x1, Pallas kernels, fields(): pl.pallas_call(field_kernel, out_shape=[jax.ShapeDtypeStruct((rows, layer...  20.7 us
    unnamed x9, local copies, waits for them, and re-layouts  3.51 us

profile of v1, /device:TPU:1, one launch (start us, length us, event | category | flops | bytes accessed | tf_op | source)
XLA Modules:
  0.0 86.9 jit_solution(18157037011895566981)
XLA Ops:
  0.6 0.0 copy-start
  0.6 0.0 copy-start.1
  0.7 0.0 copy-start.2
  0.7 20.7 %fields.1 = (f32[16,48,256]{2,1,0:T(8,128)}, bf16[8,48,256]{2,1,0:T(8,128)(2,1)}, f32[2,8,512]{2,1,0:T(8,128)}, f32[24,256]{1,0:T(8,128)}) custom-call(f32[6,256]{1,0:T(8,128)} %lat_ref.1, bf16[256,2,16,512]{3,2,1,0:T(8,128)(2,1)} %basis_ref.1, f32[2,16,512]{2,1,0:T(8,128)} %prev_ref.3, f32[2,16,512]{2,1,0:T(8,128)} %source_ref.3), custom_call_target="tpu_custom_call" | custom-call | tf_op jit(solution)/shard_map/fields/pallas_call | solution.py:161
  21.4 0.0 copy-done
  21.4 0.8 copy.14.cells_ref
  22.2 0.0 copy-done.1
  22.2 0.6 reshape.16.count_ref
  22.8 37.6 %cells.1 = (f32[24,2,16,128]{3,2,1,0:T(8,128)}, f32[8,24,128]{2,1,0:T(8,128)}) custom-call(f32[16,48,256]{2,1,0:T(8,128)} %get-tuple-element.11.own_ref, bf16[8,48,256]{2,1,0:T(8,128)(2,1)} %get-tuple-element.12.halo_ref, f32[2,8,512]{2,1,0:T(8,128)} %get-tuple-element.13.edge_ref, bf16[9,64]{1,0:T(8,128)(2,1)} %conv_in_ref.1, ...), custom_call_target="tpu_custom_call" | custom-call | tf_op jit(solution)/shard_map/cells/pallas_call | solution.py:573
  60.4 0.0 copy-done.2
  60.4 0.6 reshape.17.error_ref
  61.0 23.2 %smoother.1 = (f32[24,384]{1,0:T(8,128)}, f32[6,256]{1,0:T(8,128)}) custom-call(f32[8,24,128]{2,1,0:T(8,128)} %get-tuple-element.15.pieces_ref, f32[24,256]{1,0:T(8,128)} %get-tuple-element.16.every_ref, f32[24,384]{1,0:T(8,128)} %obs_ref.1, f32[1,384]{1,0:T(1,128)} %reshape.17.error_ref), custom_call_target="tpu_custom_call" | custom-call | tf_op jit(solution)/shard_map/smoother/pallas_call | solution.py:720
  84.2 1.4 %copy.17 = f32[24,384]{1,0:T(8,128)} copy(f32[24,384]{1,0:T(8,128)} %get-tuple-element.23) | data formatting | bytes 73728
  85.6 1.3 %copy.18 = f32[6,256]{1,0:T(8,128)} copy(f32[6,256]{1,0:T(8,128)} %get-tuple-element.24) | data formatting | bytes 12288
Async XLA Ops:
  0.6 20.8 %copy-start = (s32[384,8]{0,1:T(8,128)S(1)}, s32[384,8]{0,1:T(8,128)}, u32[]{:S(2)}) copy-start(s32[384,8]{0,1:T(8,128)} %param.18) | copy-start | bytes 36868
  0.6 21.6 %copy-start.1 = (s32[384]{0:T(512)S(1)}, s32[384]{0:T(512)}, u32[]{:S(2)}) copy-start(s32[384]{0:T(512)} %param.19) | copy-start | bytes 4612
  0.7 59.8 %copy-start.2 = (f32[384]{0:T(512)S(1)}, f32[384]{0:T(512)}, u32[]{:S(2)}) copy-start(f32[384]{0:T(512)} %param.21) | copy-start | bytes 4612

commit v2 on v1

v2 whole, which is shorter than its diff:
```python
import math

import jax
import jax.numpy as jnp
from jax import lax
from jax.experimental import pallas as pl
from jax.experimental.pallas import tpu as pltpu
from jax.sharding import PartitionSpec as P

SWEEPS = 2
STORAGE = 1.0
BF = jnp.bfloat16
F32 = jnp.float32
LANES = 128
HALO = 4
WINDOW = 32
PER_WINDOW = (WINDOW - 2) // 2
MESH = pl.DeviceIdType.MESH
BIG = 60 * 2**20


def dot(a, b):
    return jnp.dot(a, b, preferred_element_type=F32)


def dot_nt(a, b, precision=None):
    return lax.dot_general(a, b, (((1,), (1,)), ((), ())), preferred_element_type=F32, precision=precision)


def iota(shape, axis):
    return lax.broadcasted_iota(jnp.int32, shape, axis)


def ones_where(cond):
    return jnp.where(cond, 1.0, 0.0)


class Places:
    def __init__(self, side):
        self.mem, self.tile = lax.axis_index("mem"), lax.axis_index("tile")
        self.mems, self.tiles = lax.axis_size("mem"), lax.axis_size("tile")
        self.side = side
        self.plane = side * side
        self.halves = self.tiles // self.plane
        self.groups = self.mems * self.halves
        self.mine = self.mem * self.halves + self.tile // self.plane
        self.spot = lax.rem(self.tile, self.plane)

    def in_group(self, g):
        return {"mem": g // self.halves, "tile": lax.rem(g, self.halves) * self.plane + self.spot}

    def in_plane(self, at):
        return {"mem": self.mem, "tile": self.tile // self.plane * self.plane + at}


def remote(source, target, sems, index, place):
    return pltpu.make_async_remote_copy(
        src_ref=source,
        dst_ref=target,
        send_sem=sems.at[0, index],
        recv_sem=sems.at[1, index],
        device_id=place,
        device_id_type=MESH,
    )


def exchange(place, at, size, source, target, sems):
    copies = []
    for step in range(1, size):
        to = lax.rem(at + step, size)
        copies.append(remote(source(to), target.at[at], sems, step, place(to)))
        copies[-1].start()
    return copies


class RowCopies:
    def __init__(self, places, source, target, sems):
        tile, last = places.tile, places.tiles - 1
        self.has = (tile > 0, tile < last)
        to = (jnp.maximum(tile - 1, 0), jnp.minimum(tile + 1, last))
        self.copies = [
            remote(source(side), target(1 - side), sems, side, {"mem": places.mem, "tile": to[side]})
            for side in range(2)
        ]

    def start(self):
        for side in range(2):
            pl.when(self.has[side])(self.copies[side].start)

    def wait(self):
        for side in range(2):
            pl.when(self.has[side])(self.copies[side].wait_send)
            pl.when(self.has[1 - side])(self.copies[side].wait_recv)


def own_fields(every, slab, left, own_ref, mem, mems):
    members, latent = every.shape
    rows = own_ref.shape[0]
    layers = slab.shape[2]
    every = every.astype(BF).astype(F32)
    groups = latent // rows
    wide = rows * rows
    group_of = iota((1, latent), 1) // rows
    picked = jnp.concatenate([every * ones_where(group_of == g) for g in range(groups)], axis=0).astype(BF)
    spread = ones_where(lax.rem(iota((latent, wide), 0), rows) == iota((latent, wide), 1) // rows).astype(BF)
    repeated = dot(picked, spread)
    lane_row = lax.rem(iota((1, wide), 1), rows)
    for g in range(groups):
        part = repeated[g * members : (g + 1) * members]
        stacked = jnp.concatenate([part * ones_where(lane_row == r) for r in range(rows)], axis=0)
        left[:, g * wide : (g + 1) * wide] = stacked.astype(BF)
    lane = iota((1, LANES), 1)
    keep_left = (ones_where(lane >= LANES // 2) * jnp.where(mem > 0, 1.0, 0.0)).astype(BF)
    keep_right = (ones_where(lane < LANES // 2) * jnp.where(mem < mems - 1, 1.0, 0.0)).astype(BF)
    for z in range(layers):
        own = slab[0, :, z].reshape(latent * rows, LANES)
        lhs = slab[1, :, z].reshape(latent * rows, LANES)
        rhs = slab[2, :, z].reshape(latent * rows, LANES)
        both = jnp.concatenate([own, lhs * keep_left + rhs * keep_right], axis=1)
        field = dot(left[...], both).reshape(rows, members, 2 * LANES)
        own_ref[:, z * members : (z + 1) * members] = field


def decoder_weights(conv_in_ref, conv_mid_ref, conv_out_ref, taps, lift_w, mix_w, out_w, mem, mems, last):
    channels = conv_out_ref.shape[1]
    block = 4 * channels
    taps[...] = jnp.zeros_like(taps)
    taps[0:9] = conv_in_ref[...].astype(F32)
    repeat = ones_where(iota((channels, block), 0) == lax.rem(iota((channels, block), 1), channels)).astype(BF)
    in_rows = dot(taps[...].astype(BF), repeat)
    in_rows = jnp.concatenate([in_rows] * 4, axis=0)
    in_rows = (in_rows * ones_where(iota((64, block), 0) // 16 == iota((64, block), 1) // channels)).astype(BF)
    row = iota((block, 64), 0)
    col = iota((block, 64), 1)
    column = lax.rem(row, WINDOW)
    patch_row = lax.rem(row // WINDOW, 4)
    tap = lax.rem(col, 16)
    tap_row = jnp.where(tap >= 3, 1, 0) + jnp.where(tap >= 6, 1, 0)
    tap_col = tap - 3 * tap_row
    fits = (patch_row == col // 32 + tap_row) & (tap < 9)
    offset = jnp.where(fits, column - lax.rem(col // 16, 2) - tap_col, -1)
    col_of = lax.rem(iota((1, block), 1) // channels, 2)
    low, high = jnp.where(mem > 0, 1.0, 0.0), jnp.where(mem < mems - 1, 1.0, 0.0)
    for t in range(PER_WINDOW):
        weight = dot(ones_where(offset == 2 * t).astype(BF), in_rows)
        lift_w[t] = weight.astype(BF)
        if t == 0:
            lift_w[PER_WINDOW] = (weight * low).astype(BF)
        if t == 1:
            lift_w[PER_WINDOW + 1] = (weight * jnp.where(col_of == 0, low, 1.0)).astype(BF)
        if t == (last - 1) % PER_WINDOW:
            lift_w[PER_WINDOW + 2] = (weight * jnp.where(col_of == 1, high, 1.0)).astype(BF)
        if t == last % PER_WINDOW:
            lift_w[PER_WINDOW + 3] = (weight * high).astype(BF)
    mix_w[...] = jnp.zeros_like(mix_w)
    nothing = jnp.zeros((channels, channels), F32)
    for p in range(4):
        for q in range(4):
            at = ((q // 2) * 2 + p // 2) * block + ((p % 2) * 2 + q % 2) * channels
            for a in range(2):
                if not 0 <= p - a <= 2:
                    continue
                pair = [
                    conv_mid_ref[3 * (p - a) + q - b].astype(F32) if 0 <= q - b <= 2 else nothing for b in range(2)
                ]
                mix_w[at : at + channels, a * 2 * channels : (a + 1) * 2 * channels] = (
                    jnp.concatenate(pair, axis=0).T.astype(BF)
                )
    out_row = conv_out_ref[...].astype(F32)
    diag = iota((channels, channels), 0) == iota((channels, channels), 1)
    out_col = jnp.sum(jnp.where(diag, out_row, 0.0), axis=1, keepdims=True)
    out_col = jnp.concatenate([out_col] * 4, axis=0)
    group = iota((block, 2 * LANES), 0) // channels
    lane = iota((block, 2 * LANES), 1)
    match = (group // 2 == lane // LANES) & (lax.rem(group, 2) == lax.rem(lane, 2))
    out_w[...] = jnp.where(match, out_col, 0.0).astype(BF)


def pair_pieces(pieces, q, even, odd):
    lane = iota((1, LANES), 1)
    count = pieces.shape[1]

    def row_pieces(field, odd):
        own, halo = field[:, :LANES], field[:, LANES:]
        low = jnp.where(lane < LANES // 2, own, halo)
        high = jnp.where(lane < LANES // 2, halo, own)
        out = []
        for w in range(count):
            start = (WINDOW - 2) * w - HALO
            from_tile = low if w == 0 else high if w == count - 1 else own
            out.append(pltpu.roll(from_tile, (WINDOW * odd - start) % LANES, 1))
        return out

    evens, odds = row_pieces(even, 0), row_pieces(odd, 1)
    for w in range(count):
        pieces[q, w] = jnp.where(lane < WINDOW, evens[w], odds[w])


def own_windows(own_ref, pieces):
    def own_pair(q, carry):
        pair_pieces(pieces, q + HALO // 2, own_ref[2 * q], own_ref[2 * q + 1])
        return carry

    lax.fori_loop(0, own_ref.shape[0] // 2, own_pair, 0)


def all_windows(halo_ref, pieces, windows, rows):
    for half in range(HALO // 2):
        pair_pieces(pieces, half, halo_ref[2 * half].astype(F32), halo_ref[2 * half + 1].astype(F32))
        at = HALO + 2 * half
        pair_pieces(pieces, (rows + at) // 2, halo_ref[at].astype(F32), halo_ref[at + 1].astype(F32))
    lane = iota((1, LANES), 1)

    def block_row(i, carry):
        for w in range(windows.shape[0]):
            both = jnp.where(lane < LANES // 2, pieces[i, w], pltpu.roll(pieces[i + 1, w], LANES // 2, 1))
            high = both.astype(BF)
            windows[w, i] = jnp.concatenate([high, (both - high.astype(F32)).astype(BF)], axis=1)
        return carry

    lax.fori_loop(0, windows.shape[1], block_row, 0)


def convolve(windows, lift_w, mix_w, out_w, lifted, mixed, total, ends, tile, tiles, blocks):
    count, block_rows, deep, _ = windows.shape
    size = (block_rows - 1) * deep
    lane = iota((1, 2 * LANES), 1)
    pair = lax.rem(lane, LANES) // 2
    part = lane // LANES
    top = jnp.where(tile > 0, 1.0, 0.0)
    bottom = jnp.where(tile < tiles - 1, 1.0, 0.0)
    masks = {
        0: jnp.zeros((1, 2 * LANES), F32) + top,
        1: jnp.where(part == 0, top, 1.0),
        block_rows - 2: jnp.where(part == 1, bottom, 1.0),
        block_rows - 1: jnp.zeros((1, 2 * LANES), F32) + bottom,
    }

    def lift(k, slot):
        for u in range(2):
            at = jnp.minimum(2 * k + u, blocks)
            w = at // PER_WINDOW
            index = at - w * PER_WINDOW
            for special, j in enumerate((0, 1, blocks - 1, blocks)):
                index = jnp.where(at == j, PER_WINDOW + special, index)
            value = jnp.maximum(dot(windows[w].reshape(block_rows * deep, -1), lift_w[index]), 0.0)
            parts = [value[i * deep : (i + 1) * deep] for i in range(block_rows)]
            parts = [p * masks[i] if i in masks else p for i, p in enumerate(parts)]
            lifted[slot][u] = jnp.concatenate(parts, axis=0).astype(BF)

    def mix(k, slot, to):
        held = [lifted[slot].at[0], lifted[slot].at[1], lifted[(slot + 1) % 3].at[0]]
        for u in range(2):
            x, y = held[u], held[u + 1]
            lhs = jnp.concatenate([x[0:size], x[deep : deep + size], y[0:size], y[deep : deep + size]], axis=1)
            mixed[to][u] = jnp.maximum(dot(lhs, mix_w[...]), 0.0).astype(BF)

    def contract(k, at, first=False, last=False):
        even = dot(mixed[at][0], out_w[...])
        odd = dot(mixed[at][1], out_w[...])
        j = 2 * k
        if first:
            ends[...] = even
            total[...] = odd
        elif last:
            total[...] = jnp.where(pair == j - 1, even, total[...])
            ends[...] = jnp.where(pair == 0, odd, ends[...])
        else:
            total[...] = jnp.where(pair == j - 1, even, jnp.where(pair == j, odd, total[...]))

    steps = blocks // 2
    lift(0, 0)
    lift(1, 1)
    mix(0, 0, 0)
    lift(2, 2)
    contract(0, 0, first=True)
    mix(1, 1, 1)
    lift(3, 0)

    def body(q, carry):
        for v in range(6):
            k = 2 + q * 6 + v
            contract(k - 1, (1 + v) % 2)
            mix(k, (2 + v) % 3, v % 2)
            lift(k + 2, (4 + v) % 3)
        return carry

    lax.fori_loop(0, (steps - 3) // 6, body, 0)
    k = steps - 1
    contract(k - 1, (k - 1) % 2)
    mix(k, k % 3, k % 2)
    contract(k, k % 2, last=True)


def sweeps(
    own_ref, halo_ref, edge_ref, prev_ref, source_ref, total, ends, perm, first, press_ref, values,
    mem, mems, tile, tiles,
):
    rows = own_ref.shape[0]
    deep = own_ref.shape[1]
    layers = prev_ref.shape[0]
    members = deep // layers
    lane = iota((1, LANES), 1)
    top = jnp.where(tile > 0, 1.0, 0.0)
    bottom = jnp.where(tile < tiles - 1, 1.0, 0.0)
    beyond = jnp.where(lane < LANES // 2, jnp.where(mem < mems - 1, 1.0, 0.0), jnp.where(mem > 0, 1.0, 0.0))
    mine = pl.multiple_of(mem * LANES, LANES)
    before = pl.multiple_of(jnp.maximum(mem - 1, 0) * LANES, LANES)
    after = pl.multiple_of(jnp.minimum(mem + 1, mems - 1) * LANES, LANES)

    def columns(line):
        beside = jnp.where(lane < LANES // 2, line(after), line(before))
        return line(mine), beside

    def levels(pick):
        each = [columns(lambda at: pick(z, at)) for z in range(layers)]
        return [
            jnp.concatenate([jnp.broadcast_to(each[z][t], (members, LANES)) for z in range(layers)], axis=0)
            for t in range(2)
        ]

    def prev_line(index):
        r = index - 2
        if r < 0:
            return levels(lambda z, at: edge_ref[0, 2 * z + 2 + r : 2 * z + 3 + r, pl.ds(at, LANES)])
        if r >= rows:
            return levels(lambda z, at: edge_ref[1, 2 * z + r - rows : 2 * z + r - rows + 1, pl.ds(at, LANES)])
        return levels(lambda z, at: prev_ref[z, r : r + 1, pl.ds(at, LANES)])

    def source_line(index):
        r = index - 2
        if r < 0:
            return levels(lambda z, at: edge_ref[0, 4 + z : 5 + z, pl.ds(at, LANES)])
        if r >= rows:
            return levels(lambda z, at: edge_ref[1, 4 + z : 5 + z, pl.ds(at, LANES)])
        return levels(lambda z, at: source_ref[z, r : r + 1, pl.ds(at, LANES)])

    for index in range(rows + 4):
        r = index - 2
        i, a = index // 2, index % 2
        for t, parts in enumerate((total, ends)):
            value = parts[i * deep : (i + 1) * deep, a * LANES : (a + 1) * LANES]
            if 0 <= r < rows:
                field = own_ref[r, :, t * LANES : (t + 1) * LANES]
            else:
                at = HALO + r if r < 0 else HALO + r - rows
                field = halo_ref[at, :, t * LANES : (t + 1) * LANES].astype(F32)
            value = jnp.exp(field + value)
            if r < 0:
                value = jnp.where(top > 0, value, 0.0)
            if r >= rows:
                value = jnp.where(bottom > 0, value, 0.0)
            if t == 1:
                value = jnp.where(beyond > 0, value, 0.0)
            perm[index, t] = value

    def shift(own, beside, by):
        edge = LANES - 1 if by > 0 else 0
        a, b = pltpu.roll(own, -by % LANES, 1), pltpu.roll(beside, -by % LANES, 1)
        return jnp.where(lane == edge, b, a), jnp.where(lane == edge, a, b)

    def harmonic(a, b):
        both = a + b
        return jnp.where(both > 0, 2.0 * a * b / jnp.where(both > 0, both, 1.0), 0.0)

    def swap(x):
        return jnp.concatenate([x[members:], x[:members]], axis=0)

    def coefficients(index):
        here = [perm[index, t] for t in range(2)]
        right = shift(here[0], here[1], 1)
        across = [harmonic(here[t], right[t]) for t in range(2)]
        back = shift(across[0], across[1], -1)
        out = []
        for t in range(2):
            level = harmonic(here[t][:members], here[t][members:])
            out.append((across[t], back[t], jnp.concatenate([level, level], axis=0)))
        return out

    up = [harmonic(perm[0, t], perm[1, t]) for t in range(2)]
    for index in range(1, rows + 3):
        over, here, under = prev_line(index - 1), prev_line(index), prev_line(index + 1)
        down = [harmonic(perm[index, t], perm[index + 1, t]) for t in range(2)]
        coef = coefficients(index)
        right, back = shift(here[0], here[1], 1), shift(here[0], here[1], -1)
        source = source_line(index)
        for t in range(2):
            east, west, level = coef[t]
            acc = STORAGE * here[t] + source[t]
            acc = acc + down[t] * under[t] + up[t] * over[t]
            acc = acc + east * right[t] + west * back[t] + level * swap(here[t])
            first[index, t] = acc / (STORAGE + down[t] + up[t] + east + west + level)
        up = down
    up = harmonic(perm[1, 0], perm[2, 0])
    for index in range(2, rows + 2):
        r = index - 2
        down = harmonic(perm[index, 0], perm[index + 1, 0])
        east, west, level = coefficients(index)[0]
        here = first[index, 0]
        right = shift(here, first[index, 1], 1)[0]
        back = shift(here, first[index, 1], -1)[0]
        acc = STORAGE * prev_line(index)[0] + source_line(index)[0]
        acc = acc + down * first[index + 1, 0] + up * first[index - 1, 0]
        acc = acc + east * right + west * back + level * swap(here)
        press = acc / (STORAGE + down + up + east + west + level)
        up = down
        k = perm[index, 0]
        press_ref[r] = press
        for z in range(layers):
            level_press = press[z * members : (z + 1) * members]
            level_perm = k[z * members : (z + 1) * members]
            at = (z * rows + r) * LANES
            for q, value in enumerate((level_perm, level_perm * level_press)):
                high = value.astype(BF).astype(F32)
                both = jnp.concatenate([high, value - high], axis=0).astype(BF)
                values[2 * q * members : 2 * (q + 1) * members, at : at + LANES] = both


class Wells:
    def __init__(self, cells_ref, count_ref, columns, picks, places, grid_cols, grid_cells, rows):
        slots, wells = cells_ref.shape
        each = wells // places.groups
        half = LANES // 2
        ids = cells_ref[...]
        ids = jnp.where(iota((slots, wells), 0) < count_ref[...], ids, -1)
        layer = ids // grid_cells
        rest = ids - layer * grid_cells
        row = rest // grid_cols
        col = rest - row * grid_cols - places.mem * LANES
        row = row - places.tile * rows
        inside = (ids >= 0) & (row >= 0) & (row < rows) & (col >= 0) & (col < LANES)
        code = jnp.where(inside, (layer * rows + row) * LANES + col, -1)
        lane = iota((1, LANES), 1)
        tiles = []
        for t in range(places.groups // 2):
            tile = jnp.full((slots, LANES), -1, jnp.int32)
            for g in (2 * t, 2 * t + 1):
                to = half * (g % 2)
                for source in range(wells // LANES):
                    by = to - (each * g - LANES * source)
                    low, high = max(to, by), min(to + each, by + LANES)
                    if low < high:
                        moved = pltpu.roll(code[:, source * LANES : (source + 1) * LANES], by % LANES, 1)
                        tile = jnp.where((lane >= low) & (lane < high), moved, tile)
            tiles.append(tile)
        code = jnp.concatenate(tiles, axis=1)
        self.line = jnp.where(code >= 0, code // LANES, -1)
        column = jnp.where(code >= 0, lax.rem(code, LANES), -1)
        for slot in range(slots):
            columns[slot] = ones_where(iota((LANES, 1), 0) == column[slot : slot + 1]).astype(BF)
        self.columns, self.picks = columns, picks

    def fill(self, begin, end):
        slots = self.columns.shape[0]

        def each(line, carry):
            here = ones_where(self.line == line).astype(BF)
            value = self.columns[0] * here[0:1]
            for slot in range(1, slots):
                value = value + self.columns[slot] * here[slot : slot + 1]
            self.picks[pl.ds(pl.multiple_of(line * LANES, LANES), LANES)] = value
            return carry

        lax.fori_loop(begin, end, each, 0)


def main_kernel(
    lat_ref, basis_ref, prev_ref, source_ref, conv_in_ref, conv_mid_ref, conv_out_ref, cells_ref, count_ref,
    press_ref, every_ref, data_ref,
    gathered, slab, left, own, halo, send, edge, edge_send,
    taps, lift_w, mix_w, out_w, pieces, windows, l0, l1, l2, m0, m1, total, ends, perm, first, values,
    columns, picks, sums, group_in, plane_in, hold,
    slab_sems, lat_sems, edge_sems, halo_sems, group_sems, plane_sems, data_sems,
):
    side = math.isqrt(plane_in.shape[0])
    places = Places(side)
    mem, mems, tile, tiles = places.mem, places.mems, places.tile, places.tiles
    share = lat_ref.shape[0]
    members = share * mems
    layers, rows, grid_cols = prev_ref.shape
    blocks = LANES // 2 + 2

    loads = []
    for part, offset in enumerate((0, -1, 1)):
        at = jnp.clip(mem + offset, 0, mems - 1)
        loads.append(
            pltpu.make_async_copy(
                basis_ref.at[:, :, :, pl.ds(pl.multiple_of(at * LANES, LANES), LANES)],
                slab.at[part],
                slab_sems.at[part],
            )
        )
    for load in loads:
        load.start()

    barrier = pltpu.get_barrier_semaphore()
    for step in range(1, places.groups):
        to = places.in_group(lax.rem(places.mine + step, places.groups))
        pl.semaphore_signal(barrier, inc=1, device_id=to, device_id_type=MESH)
    for step in range(1, places.plane):
        to = places.in_plane(lax.rem(places.spot + step, places.plane))
        pl.semaphore_signal(barrier, inc=1, device_id=to, device_id_type=MESH)
    for ends_at, to in ((places.plane - 1, tile + 1), (0, tile - 1)):

        @pl.when((places.spot == ends_at) & (to >= 0) & (to < tiles))
        def _(to=to):
            pl.semaphore_signal(barrier, inc=1, device_id={"mem": mem, "tile": to}, device_id_type=MESH)

    decoder_weights(conv_in_ref, conv_mid_ref, conv_out_ref, taps, lift_w, mix_w, out_w, mem, mems, blocks)
    for side_at in range(2):
        begin = 0 if side_at == 0 else rows - 2
        at = 0 if side_at == 0 else rows - 1
        for z in range(layers):
            edge_send[side_at, 2 * z : 2 * z + 2] = prev_ref[z, begin : begin + 2]
            edge_send[side_at, 4 + z : 5 + z] = source_ref[z, at : at + 1]
        edge_send[side_at, 6:8] = jnp.zeros((2, grid_cols), F32)
    for side_at, at_end in ((0, tile == 0), (1, tile == tiles - 1)):

        @pl.when(at_end)
        def _(side_at=side_at):
            edge[side_at] = jnp.zeros(edge.shape[1:], F32)
            halo[side_at * HALO : (side_at + 1) * HALO] = jnp.zeros((HALO, *halo.shape[1:]), BF)

    at_last = places.spot // (places.plane - 1) * jnp.minimum(tiles - 1 - tile, 1)
    at_first = (places.plane - 1 - places.spot) // (places.plane - 1) * jnp.minimum(tile, 1)
    pl.semaphore_wait(barrier, places.groups + places.plane - 2 + at_last + at_first)

    def in_mem(at):
        return {"mem": at, "tile": tile}

    lat_copies = exchange(in_mem, mem, mems, lambda to: lat_ref, gathered, lat_sems)
    edge_copies = RowCopies(places, lambda s: edge_send.at[s], lambda s: edge.at[s], edge_sems)
    edge_copies.start()
    wells = Wells(cells_ref, count_ref, columns, picks, places, grid_cols, grid_cols * rows * tiles, rows)
    lines = layers * rows
    wells.fill(0, lines // 2)
    gathered[mem] = lat_ref[...]
    for copy in lat_copies:
        copy.wait()
    for s in range(mems):
        every_ref[share * s : share * (s + 1)] = gathered[s]
    for load in loads:
        load.wait()
    own_fields(every_ref[...], slab, left, own, mem, mems)
    send[0:HALO] = own[0:HALO].astype(BF)
    send[HALO : 2 * HALO] = own[rows - HALO : rows].astype(BF)
    halo_copies = RowCopies(
        places,
        lambda s: send.at[pl.ds(s * HALO, HALO)],
        lambda s: halo.at[pl.ds(s * HALO, HALO)],
        halo_sems,
    )
    halo_copies.start()
    own_windows(own, pieces)
    wells.fill(lines // 2, lines)
    edge_copies.wait()
    halo_copies.wait()
    all_windows(halo, pieces, windows, rows)
    convolve(windows, lift_w, mix_w, out_w, (l0, l1, l2), (m0, m1), total, ends, tile, tiles, blocks)
    sweeps(
        own, halo, edge, prev_ref, source_ref, total, ends, perm, first, press_ref, values, mem, mems, tile, tiles
    )

    got = dot(values[...], picks[...])
    weight = got[0:members] + got[members : 2 * members]
    number = got[2 * members : 3 * members] + got[3 * members : 4 * members]
    low = iota((1, LANES), 1) < LANES // 2
    for t in range(places.groups // 2):
        n, w = number[:, t * LANES : (t + 1) * LANES], weight[:, t * LANES : (t + 1) * LANES]
        sums[2 * t] = jnp.where(low, n, pltpu.roll(w, LANES // 2, 1))
        sums[2 * t + 1] = jnp.where(low, pltpu.roll(n, LANES // 2, 1), w)

    def together(target):
        value = target[0]
        for at in range(1, target.shape[0]):
            value = value + target[at]
        return value

    group_copies = exchange(places.in_group, places.mine, places.groups, lambda to: sums.at[to], group_in, group_sems)
    group_in[places.mine] = sums[places.mine]
    for copy in group_copies:
        copy.wait()
    value = together(group_in)
    hold[0] = value
    plane_in[places.spot] = value
    plane_copies = exchange(places.in_plane, places.spot, places.plane, lambda to: hold.at[0], plane_in, plane_sems)
    for copy in plane_copies:
        copy.wait()
    value = together(plane_in)
    value = value / pltpu.roll(value, LANES // 2, 1)
    hold[1] = value
    data_ref[places.mine] = value
    data_copies = exchange(places.in_group, places.mine, places.groups, lambda to: hold.at[1], data_ref, data_sems)
    for copy in data_copies:
        copy.wait()


def main(latents, basis, prev, source, conv_in, conv_mid, conv_out, perf_cells, perf_count):
    share, latent = latents.shape
    mems, tiles = lax.axis_size("mem"), lax.axis_size("tile")
    members = share * mems
    _, layers, rows, width = basis.shape
    deep = layers * members
    channels = conv_in.shape[1]
    block = 4 * channels
    blocks = LANES // 2 + 2
    count = blocks // PER_WINDOW + 1
    out_rows = rows // 2 + 2
    slots = perf_cells.shape[1]
    plane = tiles // 2
    groups = 2 * mems
    lanes = groups // 2 * LANES
    vmem = pl.BlockSpec(memory_space=pltpu.VMEM)
    piece = (members, LANES)
    return pl.pallas_call(
        main_kernel,
        out_shape=[
            jax.ShapeDtypeStruct((rows, deep, LANES), F32),
            jax.ShapeDtypeStruct((members, latent), F32),
            jax.ShapeDtypeStruct((groups, *piece), F32),
        ],
        in_specs=[vmem, pl.BlockSpec(memory_space=pl.ANY)] + [vmem] * 7,
        out_specs=[vmem] * 3,
        scratch_shapes=[
            pltpu.VMEM((mems, share, latent), F32),
            pltpu.VMEM((3, latent, layers, rows, LANES), BF),
            pltpu.VMEM((rows * members, latent * rows), BF),
            pltpu.VMEM((rows, deep, 2 * LANES), F32),
            pltpu.VMEM((2 * HALO, deep, 2 * LANES), BF),
            pltpu.VMEM((2 * HALO, deep, 2 * LANES), BF),
            pltpu.VMEM((2, 8, width), F32),
            pltpu.VMEM((2, 8, width), F32),
            pltpu.VMEM((16, channels), F32),
            pltpu.VMEM((PER_WINDOW + 4, block, block), BF),
            pltpu.VMEM((4 * block, block), BF),
            pltpu.VMEM((block, 2 * LANES), BF),
            pltpu.VMEM((rows // 2 + HALO, count, deep, LANES), F32),
            pltpu.VMEM((count, out_rows + 1, deep, 2 * LANES), BF),
        ]
        + [pltpu.VMEM((2, (out_rows + 1) * deep, block), BF)] * 3
        + [pltpu.VMEM((2, out_rows * deep, block), BF)] * 2
        + [pltpu.VMEM((out_rows * deep, 2 * LANES), F32)] * 2
        + [pltpu.VMEM((rows + 4, 2, deep, LANES), F32)] * 2
        + [
            pltpu.VMEM((4 * members, layers * rows * LANES), BF),
            pltpu.VMEM((slots, LANES, lanes), BF),
            pltpu.VMEM((layers * rows * LANES, lanes), BF),
            pltpu.VMEM((groups, *piece), F32),
            pltpu.VMEM((groups, *piece), F32),
            pltpu.VMEM((plane, *piece), F32),
            pltpu.VMEM((2, *piece), F32),
            pltpu.SemaphoreType.DMA((3,)),
            pltpu.SemaphoreType.DMA((2, mems)),
            pltpu.SemaphoreType.DMA((2, 2)),
            pltpu.SemaphoreType.DMA((2, 2)),
            pltpu.SemaphoreType.DMA((2, groups)),
            pltpu.SemaphoreType.DMA((2, plane)),
            pltpu.SemaphoreType.DMA((2, groups)),
        ],
        compiler_params=pltpu.CompilerParams(collective_id=0, has_side_effects=True, vmem_limit_bytes=BIG),
        name="main",
    )(latents, basis, prev, source, conv_in, conv_mid, conv_out.reshape(1, channels), perf_cells.T,
      perf_count.reshape(1, -1))


def update_kernel(raw_ref, data_ref, every_ref, obs_ref, error_ref, press_ref, well_ref, new_ref):
    mem, mems = lax.axis_index("mem"), lax.axis_size("mem")
    groups, members, _ = data_ref.shape
    layers = press_ref.shape[1]
    for r in range(press_ref.shape[2]):
        for z in range(layers):
            press_ref[:, z, r, :] = raw_ref[r, z * members : (z + 1) * members]
    each = obs_ref.shape[1] // groups
    lane = iota((1, LANES), 1)
    parts = []
    for t in range(obs_ref.shape[1] // LANES):
        part = jnp.zeros((members, LANES), F32)
        for g in range(groups):
            by = each * g - LANES * t
            if by <= -each or by >= LANES:
                continue
            moved = pltpu.roll(data_ref[g], by % LANES, 1)
            part = jnp.where((lane >= by) & (lane < by + each), moved, part)
        parts.append(part)
    wells = jnp.concatenate(parts, axis=1)
    well_ref[...] = wells
    scale = 2.0 * error_ref[...]
    centred = wells - jnp.sum(wells, axis=0, keepdims=True) / members
    scaled = centred / (math.sqrt(members - 1) * scale)
    innov = (obs_ref[...] - wells) / scale
    exact = lax.Precision.HIGHEST
    eye = ones_where(iota((members, members), 0) == iota((members, members), 1))
    gram = eye + dot_nt(scaled, scaled, exact)
    cross = dot_nt(innov, scaled, exact)
    work = jnp.concatenate([gram, eye], axis=1)
    row_at = iota((members, 1), 0)
    for k in range(members):
        line = work[k : k + 1] / work[k : k + 1, k : k + 1]
        work = jnp.where(row_at == k, line, work - work[:, k : k + 1] * line)
    inverse = work[:, members:]
    weights = jnp.dot(cross, inverse, preferred_element_type=F32, precision=exact)
    every = every_ref[...]
    spread = (every - jnp.sum(every, axis=0, keepdims=True) / members) / math.sqrt(members - 1)
    new = every + jnp.dot(weights, spread, preferred_element_type=F32, precision=exact)
    share = members // mems
    own = new[0:share]
    for s in range(1, mems):
        own = jnp.where(mem == s, new[s * share : (s + 1) * share], own)
    new_ref[...] = own


def update(raw, data, every, obs, error):
    rows, deep, _ = raw.shape
    _, members, _ = data.shape
    vmem = pl.BlockSpec(memory_space=pltpu.VMEM)
    return pl.pallas_call(
        update_kernel,
        out_shape=[
            jax.ShapeDtypeStruct((members, deep // members, rows, LANES), F32),
            jax.ShapeDtypeStruct(obs.shape, F32),
            jax.ShapeDtypeStruct((members // lax.axis_size("mem"), every.shape[1]), F32),
        ],
        in_specs=[vmem] * 5,
        out_specs=[vmem] * 3,
        name="update",
    )(raw, data, every, obs, error.reshape(1, -1))


def body(
    latents, basis, conv_in, conv_mid, conv_out, pressure_prev, source, perf_cells, perf_count, obs_perturbed, obs_error
):
    raw, every, data = main(
        latents, basis, pressure_prev, source, conv_in, conv_mid, conv_out, perf_cells, perf_count
    )
    return tuple(update(raw, data, every, obs_perturbed, obs_error))


def solution(mesh):
    return jax.shard_map(
        body,
        mesh=mesh,
        in_specs=(
            P("mem", None), P(None, None, "tile", None), P(), P(), P(), P(None, "tile", None), P(None, "tile", None),
            P(), P(), P(), P(),
        ),
        out_specs=(P(None, None, "tile", "mem"), P(), P("mem", None)),
        check_vma=False,
    )
```

time: 87.2 us -> 74.3 us (0.85)
  Pallas kernels: 81.6 us -> 71 us
  local copies, waits for them, and re-layouts: 4.64 us -> 2.51 us
    pallas_call x3 -> x2, Pallas kernels: 81.6 us -> 71 us  [the longest x1 66.3 us: main(): pl.pallas_call(main_kernel, out_shape=[jax.ShapeDtypeStruct((rows, deep,...]
    unnamed x9 -> x0, local copies, waits for them, and re-layouts: 3.51 us -> none
    reshape x2, local copies, waits for them, and re-layouts: 1.13 us -> 2.51 us  [the longest x1 1.26 us: update(): error.reshape(1, -1)]
where the time goes in v2:
time: 74.3 us; the launch traced here: 74.1 us
  Pallas kernels  71 us (96%)
  local copies, waits for them, and re-layouts  2.51 us (3%)
    pallas_call x1, Pallas kernels, main(): pl.pallas_call(main_kernel, out_shape=[jax.ShapeDtypeStruct((rows, deep,...  66.3 us
    pallas_call x1, Pallas kernels, update(): pl.pallas_call(update_kernel, out_shape=[jax.ShapeDtypeStruct((members, d...  4.67 us

profile of v2, /device:TPU:1, one launch (start us, length us, event | category | flops | bytes accessed | tf_op | source)
XLA Modules:
  0.0 74.1 jit_solution(8708105078203471872)
XLA Ops:
  0.6 1.2 %reshape.16.count_ref = s32[1,384]{1,0:T(1,128)} reshape(s32[384]{0:T(512)} %param.19) | data formatting | bytes 3072 | tf_op jit(solution)/shard_map/reshape | solution.py:663
  1.9 1.3 %reshape.17.error_ref = f32[1,384]{1,0:T(1,128)} reshape(f32[384]{0:T(512)} %param.21) | data formatting | bytes 3072 | tf_op jit(solution)/shard_map/reshape | solution.py:726
  3.1 66.3 %main.1 = (f32[16,48,128]{2,1,0:T(8,128)}, f32[24,256]{1,0:T(8,128)}, f32[8,24,128]{2,1,0:T(8,128)}) custom-call(f32[6,256]{1,0:T(8,128)} %lat_ref.1, bf16[256,2,16,512]{3,2,1,0:T(8,128)(2,1)} %basis_ref.1, f32[2,16,512]{2,1,0:T(8,128)} %prev_ref.1, f32[2,16,512]{2,1,0:T(8,128)} %source_ref.1, bf16[9,64]{1,0:T(8,128)(2,1)} %conv_in_ref.1, ...), custom_call_target="tpu_custom_call" | custom-call | tf_op jit(solution)/shard_map/main/pallas_call | solution.py:615
  69.5 4.7 %update.1 = (f32[24,2,16,128]{3,2,1,0:T(8,128)}, f32[24,384]{1,0:T(8,128)}, f32[6,256]{1,0:T(8,128)}) custom-call(f32[16,48,128]{2,1,0:T(8,128)} %get-tuple-element.6.raw_ref, f32[8,24,128]{2,1,0:T(8,128)} %get-tuple-element.7.data_ref, f32[24,256]{1,0:T(8,128)} %get-tuple-element.8.every_ref, f32[24,384]{1,0:T(8,128)} %obs_ref.1, f32[1,384]{1,0:T(1,128)} %reshape.17.error_ref), custom_call_target="tpu_custom_call" | custom-call | tf_op jit(solution)/shard_map/update/pallas_call | solution.py:716

commit v3 on v2

--- a/solution.py
+++ b/solution.py
@@ -121,7 +121,7 @@
         own_ref[:, z * members : (z + 1) * members] = field
 
 
-def decoder_weights(conv_in_ref, conv_mid_ref, conv_out_ref, taps, lift_w, mix_w, out_w, mem, mems, last):
+def decoder_weights(conv_in_ref, conv_mid_ref, conv_out_ref, taps, lift_w, mix_w, out_w, scale, mem, mems, last):
     channels = conv_out_ref.shape[1]
     block = 4 * channels
     taps[...] = jnp.zeros_like(taps)
@@ -167,13 +167,12 @@
                     jnp.concatenate(pair, axis=0).T.astype(BF)
                 )
     out_row = conv_out_ref[...].astype(F32)
-    diag = iota((channels, channels), 0) == iota((channels, channels), 1)
-    out_col = jnp.sum(jnp.where(diag, out_row, 0.0), axis=1, keepdims=True)
-    out_col = jnp.concatenate([out_col] * 4, axis=0)
-    group = iota((block, 2 * LANES), 0) // channels
+    scale[...] = jnp.concatenate([out_row] * 4, axis=1)
+    row = iota((block, 2 * LANES), 0)
     lane = iota((block, 2 * LANES), 1)
-    match = (group // 2 == lane // LANES) & (lax.rem(group, 2) == lax.rem(lane, 2))
-    out_w[...] = jnp.where(match, out_col, 0.0).astype(BF)
+    match = (row // LANES == lane // LANES) & (lax.rem(row // (LANES // 2), 2) == lax.rem(lane, 2))
+    match = match & (lax.rem(row // (LANES // 4), 2) == lax.rem(lane // (LANES // 2), 2))
+    out_w[...] = ones_where(match).astype(BF)
 
 
 def pair_pieces(pieces, q, even, odd):
@@ -221,11 +220,11 @@
     lax.fori_loop(0, windows.shape[1], block_row, 0)
 
 
-def convolve(windows, lift_w, mix_w, out_w, lifted, mixed, total, ends, tile, tiles, blocks):
+def convolve(windows, lift_w, mix_w, out_w, scale, lifted, mixed, total, ends, tile, tiles, blocks):
     count, block_rows, deep, _ = windows.shape
     size = (block_rows - 1) * deep
     lane = iota((1, 2 * LANES), 1)
-    pair = lax.rem(lane, LANES) // 2
+    half = lax.rem(lane, LANES // 2)
     part = lane // LANES
     top = jnp.where(tile > 0, 1.0, 0.0)
     bottom = jnp.where(tile < tiles - 1, 1.0, 0.0)
@@ -235,61 +234,73 @@
         block_rows - 2: jnp.where(part == 1, bottom, 1.0),
         block_rows - 1: jnp.zeros((1, 2 * LANES), F32) + bottom,
     }
-
-    def lift(k, slot):
+    steps = (blocks - 2) // 2
+    streams = (lambda t: 1 + t, lambda t: 1 + steps + t)
+
+    def lift(places, slot):
         for u in range(2):
-            at = jnp.minimum(2 * k + u, blocks)
-            w = at // PER_WINDOW
-            index = at - w * PER_WINDOW
-            for special, j in enumerate((0, 1, blocks - 1, blocks)):
-                index = jnp.where(at == j, PER_WINDOW + special, index)
+            at = places[u]
+            if isinstance(at, int) and at in (0, 1, blocks - 1, blocks):
+                w, index = at // PER_WINDOW, PER_WINDOW + (0, 1, blocks - 1, blocks).index(at)
+            else:
+                at = jnp.minimum(at, blocks)
+                w = at // PER_WINDOW
+                index = at - w * PER_WINDOW
+                for special, j in ((2, blocks - 1), (3, blocks)):
+                    index = jnp.where(at == j, PER_WINDOW + special, index)
             value = jnp.maximum(dot(windows[w].reshape(block_rows * deep, -1), lift_w[index]), 0.0)
             parts = [value[i * deep : (i + 1) * deep] for i in range(block_rows)]
             parts = [p * masks[i] if i in masks else p for i, p in enumerate(parts)]
             lifted[slot][u] = jnp.concatenate(parts, axis=0).astype(BF)
 
-    def mix(k, slot, to):
-        held = [lifted[slot].at[0], lifted[slot].at[1], lifted[(slot + 1) % 3].at[0]]
+    def mix(slot, to):
         for u in range(2):
-            x, y = held[u], held[u + 1]
+            x, y = lifted[slot].at[u], lifted[(slot + 1) % 3].at[u]
             lhs = jnp.concatenate([x[0:size], x[deep : deep + size], y[0:size], y[deep : deep + size]], axis=1)
-            mixed[to][u] = jnp.maximum(dot(lhs, mix_w[...]), 0.0).astype(BF)
-
-    def contract(k, at, first=False, last=False):
-        even = dot(mixed[at][0], out_w[...])
-        odd = dot(mixed[at][1], out_w[...])
-        j = 2 * k
-        if first:
-            ends[...] = even
-            total[...] = odd
-        elif last:
-            total[...] = jnp.where(pair == j - 1, even, total[...])
-            ends[...] = jnp.where(pair == 0, odd, ends[...])
-        else:
-            total[...] = jnp.where(pair == j - 1, even, jnp.where(pair == j, odd, total[...]))
-
-    steps = blocks // 2
-    lift(0, 0)
-    lift(1, 1)
-    mix(0, 0, 0)
-    lift(2, 2)
-    contract(0, 0, first=True)
-    mix(1, 1, 1)
-    lift(3, 0)
+            value = jnp.maximum(dot(lhs, mix_w[...]), 0.0) * scale[...]
+            by = LANES - LANES // 4 if u == 0 else LANES // 4
+            other = [pltpu.roll(value[:, i * LANES : (i + 1) * LANES], by, 1) for i in range(2)]
+            mixed[to][u] = (value + jnp.concatenate(other, axis=1)).astype(BF)
+
+    keep = [ones_where(half < LANES // 4).astype(BF), ones_where(half >= LANES // 4).astype(BF)]
+
+    def both_streams(at):
+        return mixed[at][0] * keep[0] + mixed[at][1] * keep[1]
+
+    def contract(t, at):
+        total[...] = jnp.where(half // 2 == t, dot(both_streams(at), out_w[...]), total[...])
+
+    def ahead(t):
+        return [stream(t) for stream in streams]
+
+    total[...] = jnp.zeros_like(total)
+    lift(ahead(0), 0)
+    lift(ahead(1), 1)
+    mix(0, 0)
+    lift(ahead(2), 2)
 
     def body(q, carry):
         for v in range(6):
-            k = 2 + q * 6 + v
-            contract(k - 1, (1 + v) % 2)
-            mix(k, (2 + v) % 3, v % 2)
-            lift(k + 2, (4 + v) % 3)
+            t = 1 + q * 6 + v
+            contract(t - 1, v % 2)
+            mix((1 + v) % 3, (1 + v) % 2)
+            lift(ahead(t + 2), v % 3)
         return carry
 
-    lax.fori_loop(0, (steps - 3) // 6, body, 0)
-    k = steps - 1
-    contract(k - 1, (k - 1) % 2)
-    mix(k, k % 3, k % 2)
-    contract(k, k % 2, last=True)
+    whole = (steps - 2) // 6
+    lax.fori_loop(0, whole, body, 0)
+    for t in range(1 + 6 * whole, steps):
+        contract(t - 1, (t - 1) % 2)
+        mix(t % 3, t % 2)
+        if t < steps - 1:
+            lift(ahead(t + 2), (t + 2) % 3)
+    contract(steps - 1, (steps - 1) % 2)
+    lift((0, blocks - 1), 0)
+    lift((1, blocks), 1)
+    mix(0, 0)
+    value = dot(both_streams(0), out_w[...])
+    swapped = [pltpu.roll(value[:, i * LANES : (i + 1) * LANES], LANES // 2, 1) for i in range(2)]
+    ends[...] = jnp.concatenate(swapped, axis=1)
 
 
 def sweeps(
@@ -422,7 +433,7 @@
         each = wells // places.groups
         half = LANES // 2
         ids = cells_ref[...]
-        ids = jnp.where(iota((slots, wells), 0) < count_ref[...], ids, -1)
+        ids = jnp.where(iota((slots, wells), 0) < count_ref[...].reshape(1, wells), ids, -1)
         layer = ids // grid_cells
         rest = ids - layer * grid_cells
         row = rest // grid_cols
@@ -467,8 +478,8 @@
 def main_kernel(
     lat_ref, basis_ref, prev_ref, source_ref, conv_in_ref, conv_mid_ref, conv_out_ref, cells_ref, count_ref,
     press_ref, every_ref, data_ref,
-    gathered, slab, left, own, halo, send, edge, edge_send,
-    taps, lift_w, mix_w, out_w, pieces, windows, l0, l1, l2, m0, m1, total, ends, perm, first, values,
+    raw, gathered, slab, left, own, halo, send, edge, edge_send,
+    taps, lift_w, mix_w, out_w, scale, pieces, windows, l0, l1, l2, m0, m1, total, ends, perm, first, values,
     columns, picks, sums, group_in, plane_in, hold,
     slab_sems, lat_sems, edge_sems, halo_sems, group_sems, plane_sems, data_sems,
 ):
@@ -506,7 +517,7 @@
         def _(to=to):
             pl.semaphore_signal(barrier, inc=1, device_id={"mem": mem, "tile": to}, device_id_type=MESH)
 
-    decoder_weights(conv_in_ref, conv_mid_ref, conv_out_ref, taps, lift_w, mix_w, out_w, mem, mems, blocks)
+    decoder_weights(conv_in_ref, conv_mid_ref, conv_out_ref, taps, lift_w, mix_w, out_w, scale, mem, mems, blocks)
     for side_at in range(2):
         begin = 0 if side_at == 0 else rows - 2
         at = 0 if side_at == 0 else rows - 1
@@ -556,9 +567,9 @@
     edge_copies.wait()
     halo_copies.wait()
     all_windows(halo, pieces, windows, rows)
-    convolve(windows, lift_w, mix_w, out_w, (l0, l1, l2), (m0, m1), total, ends, tile, tiles, blocks)
+    convolve(windows, lift_w, mix_w, out_w, scale, (l0, l1, l2), (m0, m1), total, ends, tile, tiles, blocks)
     sweeps(
-        own, halo, edge, prev_ref, source_ref, total, ends, perm, first, press_ref, values, mem, mems, tile, tiles
+        own, halo, edge, prev_ref, source_ref, total, ends, perm, first, raw, values, mem, mems, tile, tiles
     )
 
     got = dot(values[...], picks[...])
@@ -578,6 +589,9 @@
 
     group_copies = exchange(places.in_group, places.mine, places.groups, lambda to: sums.at[to], group_in, group_sems)
     group_in[places.mine] = sums[places.mine]
+    for r in range(rows):
+        for z in range(layers):
+            press_ref[:, z, r, :] = raw[r, z * members : (z + 1) * members]
     for copy in group_copies:
         copy.wait()
     value = together(group_in)
@@ -615,13 +629,14 @@
     return pl.pallas_call(
         main_kernel,
         out_shape=[
-            jax.ShapeDtypeStruct((rows, deep, LANES), F32),
+            jax.ShapeDtypeStruct((members, layers, rows, LANES), F32),
             jax.ShapeDtypeStruct((members, latent), F32),
             jax.ShapeDtypeStruct((groups, *piece), F32),
         ],
         in_specs=[vmem, pl.BlockSpec(memory_space=pl.ANY)] + [vmem] * 7,
         out_specs=[vmem] * 3,
         scratch_shapes=[
+            pltpu.VMEM((rows, deep, LANES), F32),
             pltpu.VMEM((mems, share, latent), F32),
             pltpu.VMEM((3, latent, layers, rows, LANES), BF),
             pltpu.VMEM((rows * members, latent * rows), BF),
@@ -634,6 +649,7 @@
             pltpu.VMEM((PER_WINDOW + 4, block, block), BF),
             pltpu.VMEM((4 * block, block), BF),
             pltpu.VMEM((block, 2 * LANES), BF),
+            pltpu.VMEM((1, block), F32),
             pltpu.VMEM((rows // 2 + HALO, count, deep, LANES), F32),
             pltpu.VMEM((count, out_rows + 1, deep, 2 * LANES), BF),
         ]
@@ -660,16 +676,16 @@
         compiler_params=pltpu.CompilerParams(collective_id=0, has_side_effects=True, vmem_limit_bytes=BIG),
         name="main",
     )(latents, basis, prev, source, conv_in, conv_mid, conv_out.reshape(1, channels), perf_cells.T,
-      perf_count.reshape(1, -1))
-
-
-def update_kernel(raw_ref, data_ref, every_ref, obs_ref, error_ref, press_ref, well_ref, new_ref):
+      perf_count)
+
+
+def update_kernel(
+    pressure_ref, data_ref, every_ref, obs_ref, error_ref, press_ref, well_ref, new_ref, held, load_sem, store_sem
+):
+    load = pltpu.make_async_copy(pressure_ref, held, load_sem)
+    load.start()
     mem, mems = lax.axis_index("mem"), lax.axis_size("mem")
     groups, members, _ = data_ref.shape
-    layers = press_ref.shape[1]
-    for r in range(press_ref.shape[2]):
-        for z in range(layers):
-            press_ref[:, z, r, :] = raw_ref[r, z * members : (z + 1) * members]
     each = obs_ref.shape[1] // groups
     lane = iota((1, LANES), 1)
     parts = []
@@ -684,7 +700,7 @@
         parts.append(part)
     wells = jnp.concatenate(parts, axis=1)
     well_ref[...] = wells
-    scale = 2.0 * error_ref[...]
+    scale = 2.0 * error_ref[...].reshape(1, -1)
     centred = wells - jnp.sum(wells, axis=0, keepdims=True) / members
     scaled = centred / (math.sqrt(members - 1) * scale)
     innov = (obs_ref[...] - wells) / scale
@@ -692,47 +708,61 @@
     eye = ones_where(iota((members, members), 0) == iota((members, members), 1))
     gram = eye + dot_nt(scaled, scaled, exact)
     cross = dot_nt(innov, scaled, exact)
-    work = jnp.concatenate([gram, eye], axis=1)
-    row_at = iota((members, 1), 0)
-    for k in range(members):
-        line = work[k : k + 1] / work[k : k + 1, k : k + 1]
-        work = jnp.where(row_at == k, line, work - work[:, k : k + 1] * line)
-    inverse = work[:, members:]
-    weights = jnp.dot(cross, inverse, preferred_element_type=F32, precision=exact)
     every = every_ref[...]
     spread = (every - jnp.sum(every, axis=0, keepdims=True) / members) / math.sqrt(members - 1)
-    new = every + jnp.dot(weights, spread, preferred_element_type=F32, precision=exact)
+    load.wait()
+    store = pltpu.make_async_copy(held, press_ref, store_sem)
+    store.start()
+    columns = [jnp.broadcast_to(gram[:, j : j + 1], (members, LANES)) for j in range(members)]
+    tiles = [spread[:, t * LANES : (t + 1) * LANES] for t in range(every.shape[1] // LANES)]
+    row_at = iota((members, LANES), 0)
+    for k in range(members):
+        column = columns[k]
+        inverse = 1.0 / column[k : k + 1]
+        pivot_row = row_at == k
+
+        def reduced(x):
+            line = x[k : k + 1] * inverse
+            return jnp.where(pivot_row, line, x - column * line)
+
+        for j in range(k + 1, members):
+            columns[j] = reduced(columns[j])
+        tiles = [reduced(x) for x in tiles]
+    solved = jnp.concatenate(tiles, axis=1)
+    new = every + jnp.dot(cross, solved, preferred_element_type=F32, precision=exact)
     share = members // mems
     own = new[0:share]
     for s in range(1, mems):
         own = jnp.where(mem == s, new[s * share : (s + 1) * share], own)
     new_ref[...] = own
-
-
-def update(raw, data, every, obs, error):
-    rows, deep, _ = raw.shape
+    store.wait()
+
+
+def update(press, data, every, obs, error):
     _, members, _ = data.shape
     vmem = pl.BlockSpec(memory_space=pltpu.VMEM)
+    held = pl.BlockSpec(memory_space=pl.ANY)
     return pl.pallas_call(
         update_kernel,
         out_shape=[
-            jax.ShapeDtypeStruct((members, deep // members, rows, LANES), F32),
+            jax.ShapeDtypeStruct(press.shape, F32),
             jax.ShapeDtypeStruct(obs.shape, F32),
             jax.ShapeDtypeStruct((members // lax.axis_size("mem"), every.shape[1]), F32),
         ],
-        in_specs=[vmem] * 5,
-        out_specs=[vmem] * 3,
+        in_specs=[held] + [vmem] * 4,
+        out_specs=[held] + [vmem] * 2,
+        scratch_shapes=[pltpu.VMEM(press.shape, F32), pltpu.SemaphoreType.DMA(()), pltpu.SemaphoreType.DMA(())],
         name="update",
-    )(raw, data, every, obs, error.reshape(1, -1))
+    )(press, data, every, obs, error)
 
 
 def body(
     latents, basis, conv_in, conv_mid, conv_out, pressure_prev, source, perf_cells, perf_count, obs_perturbed, obs_error
 ):
-    raw, every, data = main(
+    press, every, data = main(
         latents, basis, pressure_prev, source, conv_in, conv_mid, conv_out, perf_cells, perf_count
     )
-    return tuple(update(raw, data, every, obs_perturbed, obs_error))
+    return tuple(update(press, data, every, obs_perturbed, obs_error))
 
 
 def solution(mesh):

time: 74.3 us -> 71 us (0.956)
  local copies, waits for them, and re-layouts: 2.51 us -> 0 us
  Pallas kernels: 71 us -> 70 us
    reshape x2 -> x0, local copies, waits for them, and re-layouts: 2.51 us -> none  [the longest x1 1.26 us: update(): error.reshape(1, -1)]
    pallas_call x2, Pallas kernels: 71 us -> 70 us  [the longest x1 66.7 us: main(): pl.pallas_call(main_kernel, out_shape=[jax.ShapeDtypeStruct((members, lay...]
where the time goes in v3:
time: 71 us; the launch traced here: 70.8 us
  Pallas kernels  70 us (99%)
  between operations  0.8 us (1%)
    pallas_call x1, Pallas kernels, main(): pl.pallas_call(main_kernel, out_shape=[jax.ShapeDtypeStruct((members, lay...  66.7 us
    pallas_call x1, Pallas kernels, update(): pl.pallas_call(update_kernel, out_shape=[jax.ShapeDtypeStruct(press.shape...  3.31 us

profile of v3, /device:TPU:1, one launch (start us, length us, event | category | flops | bytes accessed | tf_op | source)
XLA Modules:
  0.0 70.8 jit_solution(3784499874225823625)
XLA Ops:
  0.6 66.7 %main.1 = (f32[24,2,16,128]{3,2,1,0:T(8,128)}, f32[24,256]{1,0:T(8,128)}, f32[8,24,128]{2,1,0:T(8,128)}) custom-call(f32[6,256]{1,0:T(8,128)} %lat_ref.1, bf16[256,2,16,512]{3,2,1,0:T(8,128)(2,1)} %basis_ref.1, f32[2,16,512]{2,1,0:T(8,128)} %prev_ref.1, f32[2,16,512]{2,1,0:T(8,128)} %source_ref.1, bf16[9,64]{1,0:T(8,128)(2,1)} %conv_in_ref.1, ...), custom_call_target="tpu_custom_call" | custom-call | tf_op jit(solution)/shard_map/main/pallas_call | solution.py:629
  67.3 3.3 %update.1 = (f32[24,2,16,128]{3,2,1,0:T(8,128)}, f32[24,384]{1,0:T(8,128)}, f32[6,256]{1,0:T(8,128)}) custom-call(f32[24,2,16,128]{3,2,1,0:T(8,128)} %get-tuple-element.6.pressure_ref, f32[8,24,128]{2,1,0:T(8,128)} %get-tuple-element.7.data_ref, f32[24,256]{1,0:T(8,128)} %get-tuple-element.8.every_ref, f32[24,384]{1,0:T(8,128)} %obs_ref.1, f32[384]{0:T(512)} %error_ref.1), custom_call_target="tpu_custom_call" | custom-call | tf_op jit(solution)/shard_map/update/pallas_call | solution.py:745

commit v4 on v3

--- a/solution.py
+++ b/solution.py
@@ -14,6 +14,7 @@
 LANES = 128
 HALO = 4
 WINDOW = 32
+EARLY = 6
 PER_WINDOW = (WINDOW - 2) // 2
 MESH = pl.DeviceIdType.MESH
 BIG = 60 * 2**20
@@ -203,11 +204,14 @@
     lax.fori_loop(0, own_ref.shape[0] // 2, own_pair, 0)
 
 
-def all_windows(halo_ref, pieces, windows, rows):
+def halo_windows(halo_ref, pieces, rows):
     for half in range(HALO // 2):
         pair_pieces(pieces, half, halo_ref[2 * half].astype(F32), halo_ref[2 * half + 1].astype(F32))
         at = HALO + 2 * half
         pair_pieces(pieces, (rows + at) // 2, halo_ref[at].astype(F32), halo_ref[at + 1].astype(F32))
+
+
+def fill_windows(pieces, windows, begin, end):
     lane = iota((1, LANES), 1)
 
     def block_row(i, carry):
@@ -217,10 +221,10 @@
             windows[w, i] = jnp.concatenate([high, (both - high.astype(F32)).astype(BF)], axis=1)
         return carry
 
-    lax.fori_loop(0, windows.shape[1], block_row, 0)
-
-
-def convolve(windows, lift_w, mix_w, out_w, scale, lifted, mixed, total, ends, tile, tiles, blocks):
+    lax.fori_loop(begin, end, block_row, 0)
+
+
+def decoder(windows, lift_w, mix_w, out_w, scale, lifted, mixed, total, ends, tile, tiles, blocks):
     count, block_rows, deep, _ = windows.shape
     size = (block_rows - 1) * deep
     lane = iota((1, 2 * LANES), 1)
@@ -236,8 +240,12 @@
     }
     steps = (blocks - 2) // 2
     streams = (lambda t: 1 + t, lambda t: 1 + steps + t)
-
-    def lift(places, slot):
+    keep = [ones_where(half < LANES // 4).astype(BF), ones_where(half >= LANES // 4).astype(BF)]
+
+    def stack(values):
+        return values[0] if len(values) == 1 else jnp.concatenate(values, axis=0)
+
+    def lift(places, slot, spans):
         for u in range(2):
             at = places[u]
             if isinstance(at, int) and at in (0, 1, blocks - 1, blocks):
@@ -248,59 +256,92 @@
                 index = at - w * PER_WINDOW
                 for special, j in ((2, blocks - 1), (3, blocks)):
                     index = jnp.where(at == j, PER_WINDOW + special, index)
-            value = jnp.maximum(dot(windows[w].reshape(block_rows * deep, -1), lift_w[index]), 0.0)
-            parts = [value[i * deep : (i + 1) * deep] for i in range(block_rows)]
-            parts = [p * masks[i] if i in masks else p for i, p in enumerate(parts)]
-            lifted[slot][u] = jnp.concatenate(parts, axis=0).astype(BF)
-
-    def mix(slot, to):
+            lhs = stack([windows[w, i : i + n + 1].reshape((n + 1) * deep, -1) for i, n in spans])
+            value = jnp.maximum(dot(lhs, lift_w[index]), 0.0)
+            done = 0
+            for first, n in spans:
+                parts = []
+                for i in range(first, first + n + 1):
+                    part = value[done : done + deep]
+                    parts.append(part * masks[i] if i in masks else part)
+                    done += deep
+                lifted[slot][u, first * deep : (first + n + 1) * deep] = stack(parts).astype(BF)
+
+    def mix(slot, to, spans):
+        operands = []
         for u in range(2):
             x, y = lifted[slot].at[u], lifted[(slot + 1) % 3].at[u]
-            lhs = jnp.concatenate([x[0:size], x[deep : deep + size], y[0:size], y[deep : deep + size]], axis=1)
-            value = jnp.maximum(dot(lhs, mix_w[...]), 0.0) * scale[...]
+            for i, n in spans:
+                here, below = slice(i * deep, (i + n) * deep), slice((i + 1) * deep, (i + n + 1) * deep)
+                operands.append(jnp.concatenate([x[here], x[below], y[here], y[below]], axis=1))
+        each = len(spans)
+        for u in range(2):
+            if each == 1:
+                value = dot(operands[u], mix_w[...])
+            else:
+                if u == 0:
+                    joined = dot(stack(operands), mix_w[...])
+                rows = joined.shape[0] // 2
+                value = joined[u * rows : (u + 1) * rows]
+            value = jnp.maximum(value, 0.0) * scale[...]
             by = LANES - LANES // 4 if u == 0 else LANES // 4
             other = [pltpu.roll(value[:, i * LANES : (i + 1) * LANES], by, 1) for i in range(2)]
-            mixed[to][u] = (value + jnp.concatenate(other, axis=1)).astype(BF)
-
-    keep = [ones_where(half < LANES // 4).astype(BF), ones_where(half >= LANES // 4).astype(BF)]
-
-    def both_streams(at):
-        return mixed[at][0] * keep[0] + mixed[at][1] * keep[1]
-
-    def contract(t, at):
-        total[...] = jnp.where(half // 2 == t, dot(both_streams(at), out_w[...]), total[...])
+            value = (value + jnp.concatenate(other, axis=1)).astype(BF)
+            done = 0
+            for i, n in spans:
+                mixed[to][u, i * deep : (i + n) * deep] = value[done : done + n * deep]
+                done += n * deep
+
+    def both_streams(at, spans):
+        parts = [mixed[at][0, i * deep : (i + n) * deep] * keep[0] + mixed[at][1, i * deep : (i + n) * deep] * keep[1]
+                 for i, n in spans]
+        return dot(stack(parts), out_w[...])
+
+    def contract(t, at, spans):
+        value = both_streams(at, spans)
+        done = 0
+        for i, n in spans:
+            rows = slice(i * deep, (i + n) * deep)
+            total[rows] = jnp.where(half // 2 == t, value[done : done + n * deep], total[rows])
+            done += n * deep
 
     def ahead(t):
         return [stream(t) for stream in streams]
 
-    total[...] = jnp.zeros_like(total)
-    lift(ahead(0), 0)
-    lift(ahead(1), 1)
-    mix(0, 0)
-    lift(ahead(2), 2)
-
-    def body(q, carry):
-        for v in range(6):
-            t = 1 + q * 6 + v
-            contract(t - 1, v % 2)
-            mix((1 + v) % 3, (1 + v) % 2)
-            lift(ahead(t + 2), v % 3)
-        return carry
-
-    whole = (steps - 2) // 6
-    lax.fori_loop(0, whole, body, 0)
-    for t in range(1 + 6 * whole, steps):
-        contract(t - 1, (t - 1) % 2)
-        mix(t % 3, t % 2)
-        if t < steps - 1:
-            lift(ahead(t + 2), (t + 2) % 3)
-    contract(steps - 1, (steps - 1) % 2)
-    lift((0, blocks - 1), 0)
-    lift((1, blocks), 1)
-    mix(0, 0)
-    value = dot(both_streams(0), out_w[...])
-    swapped = [pltpu.roll(value[:, i * LANES : (i + 1) * LANES], LANES // 2, 1) for i in range(2)]
-    ends[...] = jnp.concatenate(swapped, axis=1)
+    def run(begin, end, spans, last=()):
+        lift(ahead(begin), 0, spans)
+        lift(ahead(begin + 1), 1, spans)
+        mix(0, 0, spans)
+        lift(ahead(begin + 2), 2, spans)
+        whole = (end - begin - 2) // 6
+
+        def body(q, carry):
+            for v in range(6):
+                t = begin + 1 + q * 6 + v
+                contract(t - 1, v % 2, spans)
+                mix((1 + v) % 3, (1 + v) % 2, spans)
+                lift(ahead(t + 2), v % 3, spans)
+            return carry
+
+        if whole:
+            lax.fori_loop(0, whole, body, 0)
+        for step in range(1 + 6 * whole, end - begin):
+            contract(begin + step - 1, (step - 1) % 2, spans)
+            mix(step % 3, step % 2, spans)
+            if step < end - begin - 1:
+                lift(ahead(begin + step + 2), (step + 2) % 3, spans)
+        final = end - begin - 1
+        if last:
+            lift((0, blocks - 1), (final + 2) % 3, last)
+            lift((1, blocks), final % 3, last)
+            mix((final + 2) % 3, (final + 1) % 2, last)
+        contract(end - 1, final % 2, spans)
+        if last:
+            value = both_streams((final + 1) % 2, last)
+            swapped = [pltpu.roll(value[:, i * LANES : (i + 1) * LANES], LANES // 2, 1) for i in range(2)]
+            ends[...] = jnp.concatenate(swapped, axis=1)
+
+    return run, steps
 
 
 def sweeps(
@@ -544,7 +585,7 @@
     edge_copies.start()
     wells = Wells(cells_ref, count_ref, columns, picks, places, grid_cols, grid_cols * rows * tiles, rows)
     lines = layers * rows
-    wells.fill(0, lines // 2)
+    wells.fill(0, lines)
     gathered[mem] = lat_ref[...]
     for copy in lat_copies:
         copy.wait()
@@ -563,11 +604,21 @@
     )
     halo_copies.start()
     own_windows(own, pieces)
-    wells.fill(lines // 2, lines)
+    inner = HALO // 2
+    outer = rows // 2 + inner
+    fill_windows(pieces, windows, inner, outer - 1)
+    run, steps = decoder(
+        windows, lift_w, mix_w, out_w, scale, (l0, l1, l2), (m0, m1), total, ends, tile, tiles, blocks
+    )
+    total[...] = jnp.zeros_like(total)
+    run(0, EARLY, ((inner, rows // 2 - 2),))
     edge_copies.wait()
     halo_copies.wait()
-    all_windows(halo, pieces, windows, rows)
-    convolve(windows, lift_w, mix_w, out_w, scale, (l0, l1, l2), (m0, m1), total, ends, tile, tiles, blocks)
+    halo_windows(halo, pieces, rows)
+    fill_windows(pieces, windows, 0, inner)
+    fill_windows(pieces, windows, outer - 1, outer + 1)
+    run(0, EARLY, ((0, inner), (outer - 2, inner)))
+    run(EARLY, steps, ((0, outer),), last=((0, outer),))
     sweeps(
         own, halo, edge, prev_ref, source_ref, total, ends, perm, first, raw, values, mem, mems, tile, tiles
     )

time: 71 us -> 69.4 us (0.977)
  Pallas kernels: 70 us -> 68.4 us
    pallas_call x1, Pallas kernels: 66.7 us -> 65.1 us  [main(): pl.pallas_call(main_kernel, out_shape=[jax.ShapeDtypeStruct((members, lay...]
where the time goes in v4:
time: 69.4 us; the launch traced here: 69.2 us
  Pallas kernels  68.4 us (99%)
  between operations  0.8 us (1%)
    pallas_call x1, Pallas kernels, main(): pl.pallas_call(main_kernel, out_shape=[jax.ShapeDtypeStruct((members, lay...  65.1 us
    pallas_call x1, Pallas kernels, update(): pl.pallas_call(update_kernel, out_shape=[jax.ShapeDtypeStruct(press.shape...  3.31 us

profile of v4, /device:TPU:1, one launch (start us, length us, event | category | flops | bytes accessed | tf_op | source)
XLA Modules:
  0.0 69.2 jit_solution(17207396474303872613)
XLA Ops:
  0.6 65.1 %main.1 = (f32[24,2,16,128]{3,2,1,0:T(8,128)}, f32[24,256]{1,0:T(8,128)}, f32[8,24,128]{2,1,0:T(8,128)}) custom-call(f32[6,256]{1,0:T(8,128)} %lat_ref.1, bf16[256,2,16,512]{3,2,1,0:T(8,128)(2,1)} %basis_ref.1, f32[2,16,512]{2,1,0:T(8,128)} %prev_ref.1, f32[2,16,512]{2,1,0:T(8,128)} %source_ref.1, bf16[9,64]{1,0:T(8,128)(2,1)} %conv_in_ref.1, ...), custom_call_target="tpu_custom_call" | custom-call | tf_op jit(solution)/shard_map/main/pallas_call | solution.py:680
  65.7 3.3 %update.1 = (f32[24,2,16,128]{3,2,1,0:T(8,128)}, f32[24,384]{1,0:T(8,128)}, f32[6,256]{1,0:T(8,128)}) custom-call(f32[24,2,16,128]{3,2,1,0:T(8,128)} %get-tuple-element.6.pressure_ref, f32[8,24,128]{2,1,0:T(8,128)} %get-tuple-element.7.data_ref, f32[24,256]{1,0:T(8,128)} %get-tuple-element.8.every_ref, f32[24,384]{1,0:T(8,128)} %obs_ref.1, f32[384]{0:T(512)} %error_ref.1), custom_call_target="tpu_custom_call" | custom-call | tf_op jit(solution)/shard_map/update/pallas_call | solution.py:796

commit v5 on v4

--- a/solution.py
+++ b/solution.py
@@ -14,10 +14,11 @@
 LANES = 128
 HALO = 4
 WINDOW = 32
-EARLY = 6
+EARLY = 4
 PER_WINDOW = (WINDOW - 2) // 2
 MESH = pl.DeviceIdType.MESH
 BIG = 60 * 2**20
+TINY = 2.0**-126
 
 
 def dot(a, b):
@@ -412,8 +413,7 @@
         return jnp.where(lane == edge, b, a), jnp.where(lane == edge, a, b)
 
     def harmonic(a, b):
-        both = a + b
-        return jnp.where(both > 0, 2.0 * a * b / jnp.where(both > 0, both, 1.0), 0.0)
+        return 2.0 * a * b / jnp.maximum(a + b, TINY)
 
     def swap(x):
         return jnp.concatenate([x[members:], x[:members]], axis=0)
@@ -436,7 +436,7 @@
         coef = coefficients(index)
         right, back = shift(here[0], here[1], 1), shift(here[0], here[1], -1)
         source = source_line(index)
-        for t in range(2):
+        for t in range(2 if 2 <= index < rows + 2 else 1):
             east, west, level = coef[t]
             acc = STORAGE * here[t] + source[t]
             acc = acc + down[t] * under[t] + up[t] * over[t]

time: 69.4 us -> 69.5 us (level)
  no operation moved by 1% of the time
where the time goes in v5:
time: 69.5 us; the launch traced here: 69.3 us
  Pallas kernels  68.5 us (99%)
  between operations  0.8 us (1%)
    pallas_call x1, Pallas kernels, main(): pl.pallas_call(main_kernel, out_shape=[jax.ShapeDtypeStruct((members, lay...  65.2 us
    pallas_call x1, Pallas kernels, update(): pl.pallas_call(update_kernel, out_shape=[jax.ShapeDtypeStruct(press.shape...  3.31 us

profile of v5, /device:TPU:1, one launch (start us, length us, event | category | flops | bytes accessed | tf_op | source)
XLA Modules:
  0.0 69.3 jit_solution(13134981320826121988)
XLA Ops:
  0.6 65.2 %main.1 = (f32[24,2,16,128]{3,2,1,0:T(8,128)}, f32[24,256]{1,0:T(8,128)}, f32[8,24,128]{2,1,0:T(8,128)}) custom-call(f32[6,256]{1,0:T(8,128)} %lat_ref.1, bf16[256,2,16,512]{3,2,1,0:T(8,128)(2,1)} %basis_ref.1, f32[2,16,512]{2,1,0:T(8,128)} %prev_ref.1, f32[2,16,512]{2,1,0:T(8,128)} %source_ref.1, bf16[9,64]{1,0:T(8,128)(2,1)} %conv_in_ref.1, ...), custom_call_target="tpu_custom_call" | custom-call | tf_op jit(solution)/shard_map/main/pallas_call | solution.py:680
  65.8 3.3 %update.1 = (f32[24,2,16,128]{3,2,1,0:T(8,128)}, f32[24,384]{1,0:T(8,128)}, f32[6,256]{1,0:T(8,128)}) custom-call(f32[24,2,16,128]{3,2,1,0:T(8,128)} %get-tuple-element.6.pressure_ref, f32[8,24,128]{2,1,0:T(8,128)} %get-tuple-element.7.data_ref, f32[24,256]{1,0:T(8,128)} %get-tuple-element.8.every_ref, f32[24,384]{1,0:T(8,128)} %obs_ref.1, f32[384]{0:T(512)} %error_ref.1), custom_call_target="tpu_custom_call" | custom-call | tf_op jit(solution)/shard_map/update/pallas_call | solution.py:796
